TPU v7x, 32 devices: a whole 2x2x4 slice. The times are simulated.
32 devices in a mesh: dp: 8 (over y, x, core), expert: 4 (over z).
Axes of the slice: x: 2, y: 2, z: 4, core: 2. Of those that a mesh axis runs over, the one named last changes fastest.
Arguments:
- tokens: bfloat16 [12288, 1024], P(('dp', 'expert')), may hold values from -6 to 6
- cotangent: bfloat16 [12288, 1024], P(('dp', 'expert')), may hold values from -6 to 6
- routes: int32 [12288, 8], P(('dp', 'expert')), may hold values from 0 to 15, all different within a row; in each aligned block of 384 rows (0 to 383, 384 to 767, ...) at most 256 rows name the same one
- cont_ids: int32 [32, 128], P(('dp', 'expert')), may hold values from 0 to 1, never falling along the last dimension, each value on 1 to 96 neighbouring positions
- norm_gains: float32 [1024, 2], replicated, may hold values from 0.5 to 1.5
- gains_moment: float32 [1024, 2], P(('dp', 'expert')), may hold values from -192 to 192
- gains_average: float32 [1024, 2], P(('dp', 'expert')), may hold values from 0.5 to 1.5
- heads_in: bfloat16 [1024, 2048], replicated, may hold values from -0.5 to 0.5
- heads_in_master: float32 [1024, 2048], P(('dp', 'expert')), may hold values from -0.625 to 0.625
- heads_in_moment: float32 [1024, 2048], P(('dp', 'expert')), may hold values from -128 to 128
- heads_in_average: float32 [1024, 2048], P(('dp', 'expert')), may hold values from -0.625 to 0.625
- heads_out: bfloat16 [1024, 1024], replicated, may hold values from -1.5 to 1.5
- heads_out_master: float32 [1024, 1024], P(('dp', 'expert')), may hold values from -0.1875 to 0.1875
- heads_out_moment: float32 [1024, 1024], P(('dp', 'expert')), may hold values from -32 to 32
- heads_out_average: float32 [1024, 1024], P(('dp', 'expert')), may hold values from -0.1875 to 0.1875
- router: bfloat16 [1024, 16], replicated, may hold values from -0.09375 to 0.09375
- router_master: float32 [1024, 16], P(('dp', 'expert')), may hold values from -2.5 to 2.5
- router_moment: float32 [1024, 16], P(('dp', 'expert')), may hold values from -128 to 128
- router_average: float32 [1024, 16], P(('dp', 'expert')), may hold values from -2.5 to 2.5
- expert_in: bfloat16 [16, 1024, 1024], P('expert'), may hold values from -0.1875 to 0.1875
- expert_in_master: float32 [16, 1024, 1024], P('expert', 'dp'), may hold values from -0.25 to 0.25
- expert_in_moment: float32 [16, 1024, 1024], P('expert', 'dp'), may hold values from -16 to 16
- expert_in_average: float32 [16, 1024, 1024], P('expert', 'dp'), may hold values from -0.25 to 0.25
- expert_out: bfloat16 [16, 1024, 512], P('expert'), may hold values from -1 to 1
- expert_out_master: float32 [16, 1024, 512], P('expert', 'dp'), may hold values from -0.0546875 to 0.0546875
- expert_out_moment: float32 [16, 1024, 512], P('expert', 'dp'), may hold values from -3.5 to 3.5
- expert_out_average: float32 [16, 1024, 512], P('expert', 'dp'), may hold values from -0.0546875 to 0.0546875
Outputs:
- output: bfloat16 [12288, 1024], P(('dp', 'expert'))
- token_grad: float32 [12288, 1024], P(('dp', 'expert'))
- gains_next: float32 [1024, 2], P(('dp', 'expert'))
- gains_moment_next: float32 [1024, 2], P(('dp', 'expert'))
- gains_average_next: float32 [1024, 2], P(('dp', 'expert'))
- heads_in_next: float32 [1024, 2048], P(('dp', 'expert'))
- heads_in_moment_next: float32 [1024, 2048], P(('dp', 'expert'))
- heads_in_average_next: float32 [1024, 2048], P(('dp', 'expert'))
- heads_out_next: float32 [1024, 1024], P(('dp', 'expert'))
- heads_out_moment_next: float32 [1024, 1024], P(('dp', 'expert'))
- heads_out_average_next: float32 [1024, 1024], P(('dp', 'expert'))
- router_next: float32 [1024, 16], P(('dp', 'expert'))
- router_moment_next: float32 [1024, 16], P(('dp', 'expert'))
- router_average_next: float32 [1024, 16], P(('dp', 'expert'))
- expert_in_next: float32 [16, 1024, 1024], P('expert', 'dp')
- expert_in_moment_next: float32 [16, 1024, 1024], P('expert', 'dp')
- expert_in_average_next: float32 [16, 1024, 1024], P('expert', 'dp')
- expert_out_next: float32 [16, 1024, 512], P('expert', 'dp')
- expert_out_moment_next: float32 [16, 1024, 512], P('expert', 'dp')
- expert_out_average_next: float32 [16, 1024, 512], P('expert', 'dp')
Inputs may be any that keep to these rules, and one draw needn't show every extreme that they name: `routes`: each row names 8 different experts. Among the tokens of one group no expert is named more than 256 times, a bound that some block reaches. `cont_ids`: in each row the numbers never fall; each of the 2 continuations has 1 to 96 tokens.
All inputs are finite; a program needn't handle non-finite values.
Results may differ from a plain program's by a relative error of at most 0.017.
Values may be sent and summed in bfloat16 or wider, within the bound.
A program may use at most 256 MiB of HBM per device.

v0:
```python
import functools

import jax
import jax.numpy as jnp
from jax import lax
from jax.experimental import pallas as pl
from jax.experimental.pallas import tpu as pltpu
from jax.sharding import PartitionSpec as P

HEADS = 16
KV_HEADS = 8
HEAD_DIM = 64


EPS = 1e-06
SCALE = 0.015625
THETA = 10000.0
MOMENTUM = 0.9
DECAY = 0.8
RATE = 0.001
HIGHEST = lax.Precision.HIGHEST


def layout(labels_row, prompt_len):
    places = jnp.arange(prompt_len + labels_row.shape[0], dtype=jnp.int32)
    earlier = jnp.sum((labels_row[None, :] < labels_row[:, None]).astype(jnp.int32), axis=1)
    offset = places[prompt_len:] - prompt_len - earlier
    positions = jnp.concatenate([places[:prompt_len], prompt_len + offset]).astype(jnp.float32)
    labels = jnp.concatenate([jnp.full((prompt_len,), -1, jnp.int32), labels_row])
    allowed = (places[None, :] <= places[:, None]) & (
        (places[None, :] < prompt_len) | (labels[None, :] == labels[:, None])
    )
    return (positions, allowed)


def rope_tables(positions):
    middle = HEAD_DIM // 2
    frequency = THETA ** (-2.0 * jnp.arange(middle, dtype=jnp.float32) / HEAD_DIM)
    angles = positions[:, None] * frequency[None, :]
    cosine, sine = jnp.cos(angles), jnp.sin(angles)
    return (
        jnp.concatenate([cosine] * 4, axis=1),
        jnp.concatenate([-sine, sine, -sine, sine], axis=1),
    )


def update(gradient, master, moment, average):
    moment_next = MOMENTUM * moment + gradient
    master_next = master - RATE * (gradient + MOMENTUM * moment_next)
    return (master_next, moment_next, DECAY * average + (1.0 - DECAY) * master_next)


F32 = jnp.float32
BF16 = jnp.bfloat16
MESH = pl.DeviceIdType.MESH
VMEM_MOST = 60 * 2**20


def contract(left, right, left_axis, right_axis):
    return lax.dot_general(
        left, right, (((left_axis,), (right_axis,)), ((), ())), preferred_element_type=F32
    )


def visit_order(line):
    return [sorted(range(line), key=lambda s: (abs(s - z), s)) for z in range(line)]


def pick(table, row, column):
    value = jnp.int32(table[0][0])
    for r in range(len(table)):
        for c in range(len(table[0])):
            value = jnp.where((row == r) & (column == c), jnp.int32(table[r][c]), value)
    return value


def bank_kernel(
    line,
    rows_hbm,
    cots_hbm,
    gates_hbm,
    up_hbm,
    down_hbm,
    mix_hbm,
    back_hbm,
    gate_grads_hbm,
    gated_hbm,
    inner_hbm,
    rows_all_hbm,
    rows,
    cots,
    gates,
    gate_grads,
    gate_grads_sent,
    up,
    down,
    mix_sum,
    back_sum,
    stage,
    gated,
    inner,
    columns,
    row_send,
    row_recv,
    gate_send,
    gate_recv,
    weight_sem,
    local_sem,
    out_sem,
    grad_send,
    grad_recv,
):
    dp = lax.axis_index("dp")
    z = lax.axis_index("expert")
    experts, width, ff_width = down.shape

    def weight_copies(e):
        return (
            pltpu.make_async_copy(up_hbm.at[e], up.at[e], weight_sem.at[0, e]),
            pltpu.make_async_copy(down_hbm.at[e], down.at[e], weight_sem.at[1, e]),
        )

    for e in range(experts):
        for copy in weight_copies(e):
            copy.start()
    own_rows = pltpu.make_async_copy(rows_hbm, rows.at[z], local_sem.at[0])
    own_rows.start()
    all_cots = pltpu.make_async_copy(cots_hbm, cots, local_sem.at[1])
    all_cots.start()
    own_gates = pltpu.make_async_copy(gates_hbm.at[z], gates.at[z], local_sem.at[2])
    own_gates.start()

    barrier = pltpu.get_barrier_semaphore()
    for step in range(1, line):
        pl.semaphore_signal(
            barrier, inc=1, device_id=(dp, lax.rem(z + step, line)), device_id_type=MESH
        )
    pl.semaphore_wait(barrier, line - 1)

    def row_copy(source, block, sem, target):
        return pltpu.make_async_remote_copy(
            src_ref=source,
            dst_ref=rows.at[block],
            send_sem=row_send.at[sem],
            recv_sem=row_recv.at[block],
            device_id=(dp, target),
            device_id_type=MESH,
        )

    @pl.when(z < line - 1)
    def _():
        row_copy(rows_hbm, z, line, z + 1).start()

    @pl.when(z > 0)
    def _():
        row_copy(rows_hbm, z, line + 1, z - 1).start()

    def gate_copy(step):
        peer = lax.rem(z + step, line)
        return pltpu.make_async_remote_copy(
            src_ref=gates_hbm.at[peer],
            dst_ref=gates.at[z],
            send_sem=gate_send.at[step],
            recv_sem=gate_recv.at[step],
            device_id=(dp, peer),
            device_id_type=MESH,
        )

    for step in range(1, line):
        gate_copy(step).start()
    own_rows.wait()
    all_cots.wait()
    own_gates.wait()
    for step in range(1, line):
        gate_copy(step).wait()

    order = visit_order(line)

    def out_copies(slot, block):
        return (
            pltpu.make_async_copy(stage.at[slot, 0], mix_hbm.at[block], out_sem.at[slot, 0]),
            pltpu.make_async_copy(stage.at[slot, 1], back_hbm.at[block], out_sem.at[slot, 1]),
            pltpu.make_async_copy(gated.at[slot], gated_hbm.at[block], out_sem.at[slot, 2]),
            pltpu.make_async_copy(inner.at[slot], inner_hbm.at[block], out_sem.at[slot, 3]),
        )

    def grad_copy(block, step):
        return pltpu.make_async_remote_copy(
            src_ref=gate_grads_sent.at[block],
            dst_ref=gate_grads.at[z],
            send_sem=grad_send.at[block],
            recv_sem=grad_recv.at[z],
            device_id=(dp, block),
            device_id_type=MESH,
        )

    def visit(k, _):
        block = pick(order, z, k)
        slot = lax.rem(k, 2)
        apart = jnp.abs(block - z)
        previous = pick(order, z, jnp.maximum(k - 1, 0))
        first = (k > 0) & (apart != jnp.abs(previous - z))
        below = z - apart
        above = z + apart

        @pl.when(first & (below >= 0))
        def _():
            low = jnp.maximum(below, 0)
            row_copy(rows_hbm, low, low, z).wait_recv()

            @pl.when(z < line - 1)
            def _():
                row_copy(rows.at[low], low, low, z + 1).start()

        @pl.when(first & (above < line))
        def _():
            high = jnp.minimum(above, line - 1)
            row_copy(rows_hbm, high, high, z).wait_recv()

            @pl.when(z > 0)
            def _():
                row_copy(rows.at[high], high, high, z - 1).start()

        @pl.when(k >= 2)
        def _():
            for copy in out_copies(slot, pick(order, z, jnp.maximum(k - 2, 0))):
                copy.wait()

        mix_sum[...] = jnp.zeros_like(mix_sum)
        back_sum[...] = jnp.zeros_like(back_sum)
        columns[...] = jnp.zeros_like(columns)
        gate_columns = gates[block].T
        lane = lax.broadcasted_iota(jnp.int32, gate_columns.shape, 1)
        wide_lane = lax.broadcasted_iota(jnp.int32, columns.shape, 1)

        def expert(e, _):
            @pl.when(k == 0)
            def _():
                for copy in weight_copies(e):
                    copy.wait()

            gate_col = jnp.sum(jnp.where(lane == e, gate_columns, 0.0), axis=1, keepdims=True)
            both = contract(rows[block], up[e], 1, 0)
            returned = contract(cots[block], down[e], 1, 0)
            gate_part = both[:, :ff_width]
            up_part = both[:, ff_width:]
            sigmoid_gate = jax.nn.sigmoid(gate_part)
            silu_gate = gate_part * sigmoid_gate
            active = silu_gate * up_part
            gated_part = (active * gate_col).astype(BF16)
            gated[slot, :, pl.ds(pl.multiple_of(e * ff_width, ff_width), ff_width)] = gated_part
            mix_sum[...] += contract(gated_part, down[e], 1, 1)
            gate_grad = jnp.sum(active * returned, axis=1, keepdims=True)
            columns[...] = jnp.where(wide_lane == e, gate_grad, columns[...])
            scaled = returned * gate_col
            grad_gate = scaled * up_part * (sigmoid_gate * (1.0 + gate_part * (1.0 - sigmoid_gate)))
            grad_up = scaled * silu_gate
            grads = jnp.concatenate([grad_gate, grad_up], axis=1).astype(BF16)
            inner[slot, :, pl.ds(pl.multiple_of(e * 2 * ff_width, ff_width), 2 * ff_width)] = grads
            back_sum[...] += contract(grads, up[e], 1, 1)
            return 0

        lax.fori_loop(0, experts, expert, 0)
        stage[slot, 0] = mix_sum[...].astype(BF16)
        stage[slot, 1] = back_sum[...].astype(BF16)
        for copy in out_copies(slot, block):
            copy.start()
        gate_grads_sent[block] = columns[...].T[: gate_grads.shape[1]]

        @pl.when(block == z)
        def _():
            gate_grads[z] = gate_grads_sent[z]

        @pl.when(block != z)
        def _():
            grad_copy(block, 0).start()

        return 0

    lax.fori_loop(0, line, visit, 0)
    for k in (line - 2, line - 1):
        for copy in out_copies(k % 2, pick(order, z, k)):
            copy.wait()

    @pl.when(z < line - 1)
    def _():
        row_copy(rows_hbm, z, line, z + 1).wait_send()

    @pl.when(z > 0)
    def _():
        row_copy(rows_hbm, z, line + 1, z - 1).wait_send()

    for s in range(line):

        @pl.when(((s < z) & (z < line - 1)) | ((s > z) & (z > 0)))
        def _(s=s):
            row_copy(rows_hbm, s, s, z).wait_send()

        @pl.when(s != z)
        def _(s=s):
            grad_copy(s, 0).wait_send()
            pltpu.make_async_remote_copy(
                src_ref=gate_grads_sent.at[s],
                dst_ref=gate_grads.at[s],
                send_sem=grad_send.at[s],
                recv_sem=grad_recv.at[s],
                device_id=(dp, z),
                device_id_type=MESH,
            ).wait_recv()

    last = (
        pltpu.make_async_copy(rows, rows_all_hbm, local_sem.at[0]),
        pltpu.make_async_copy(gate_grads, gate_grads_hbm, local_sem.at[1]),
    )
    for copy in last:
        copy.start()
    for copy in last:
        copy.wait()


def bank(rows, cots, gates, up, down, line):
    tokens, width = rows.shape
    experts, _, ff_width = down.shape
    shape = jax.ShapeDtypeStruct
    held = gates.shape[1:]
    anywhere = pl.BlockSpec(memory_space=pl.ANY)
    work = 10 * line * tokens * experts * width * ff_width
    return pl.pallas_call(
        functools.partial(bank_kernel, line),
        out_shape=(
            shape((line, tokens, width), BF16),
            shape((line, tokens, width), BF16),
            shape((line,) + held, F32),
            shape((line, tokens, experts * ff_width), BF16),
            shape((line, tokens, experts * 2 * ff_width), BF16),
            shape((line, tokens, width), BF16),
        ),
        in_specs=[anywhere] * 5,
        out_specs=(anywhere,) * 6,
        scratch_shapes=[
            pltpu.VMEM((line, tokens, width), BF16),
            pltpu.VMEM((line, tokens, width), BF16),
            pltpu.VMEM((line,) + held, F32),
            pltpu.VMEM((line,) + held, F32),
            pltpu.VMEM((line,) + held, F32),
            pltpu.VMEM(up.shape, BF16),
            pltpu.VMEM(down.shape, BF16),
            pltpu.VMEM((tokens, width), F32),
            pltpu.VMEM((tokens, width), F32),
            pltpu.VMEM((2, 2, tokens, width), BF16),
            pltpu.VMEM((2, tokens, experts * ff_width), BF16),
            pltpu.VMEM((2, tokens, experts * 2 * ff_width), BF16),
            pltpu.VMEM((tokens, 128), F32),
            pltpu.SemaphoreType.DMA((line + 2,)),
            pltpu.SemaphoreType.DMA((line,)),
            pltpu.SemaphoreType.DMA((line,)),
            pltpu.SemaphoreType.DMA((line,)),
            pltpu.SemaphoreType.DMA((2, experts)),
            pltpu.SemaphoreType.DMA((3,)),
            pltpu.SemaphoreType.DMA((2, 4)),
            pltpu.SemaphoreType.DMA((line,)),
            pltpu.SemaphoreType.DMA((line,)),
        ],
        compiler_params=pltpu.CompilerParams(
            collective_id=1, has_side_effects=True, vmem_limit_bytes=VMEM_MOST
        ),
        cost_estimate=pl.CostEstimate(flops=work, bytes_accessed=2**26, transcendentals=0),
    )(rows, cots, gates, up, down)


def weight_grads_kernel(rows, cots, gated, inner, up_grad, down_grad):
    step = 256
    for at in range(0, rows.shape[1], step):
        up_grad[0, at : at + step] = contract(rows[:, at : at + step], inner[...], 0, 0).astype(BF16)
        down_grad[0, at : at + step] = contract(cots[:, at : at + step], gated[...], 0, 0).astype(
            BF16
        )


def weight_grads(rows, cots, gated, inner, experts):
    tokens, width = rows.shape
    ff_width = gated.shape[1] // experts
    whole = pl.BlockSpec((tokens, width), lambda e: (0, 0))
    return pl.pallas_call(
        weight_grads_kernel,
        grid=(experts,),
        out_shape=(
            jax.ShapeDtypeStruct((experts, width, 2 * ff_width), BF16),
            jax.ShapeDtypeStruct((experts, width, ff_width), BF16),
        ),
        in_specs=[
            whole,
            whole,
            pl.BlockSpec((tokens, ff_width), lambda e: (0, e)),
            pl.BlockSpec((tokens, 2 * ff_width), lambda e: (0, e)),
        ],
        out_specs=(
            pl.BlockSpec((1, width, 2 * ff_width), lambda e: (e, 0, 0)),
            pl.BlockSpec((1, width, ff_width), lambda e: (e, 0, 0)),
        ),
        compiler_params=pltpu.CompilerParams(vmem_limit_bytes=VMEM_MOST),
        cost_estimate=pl.CostEstimate(
            flops=6 * tokens * width * experts * ff_width,
            bytes_accessed=2 * tokens * (2 * width + 3 * experts * ff_width)
            + 6 * experts * width * ff_width,
            transcendentals=0,
        ),
    )(rows, cots, gated, inner)


def bank_grads_kernel(
    rows_hbm,
    cots_hbm,
    gated_hbm,
    inner_hbm,
    sum_hbm,
    rows,
    cots,
    gated,
    inner,
    grads,
    core_sum,
    first_sum,
    last_sum,
    total,
    load_sem,
    send_sem,
    recv_sem,
    out_sem,
):
    experts = grads.shape[0]
    ff_width = gated.shape[2]
    block_rows = grads.shape[4]
    dp = lax.axis_index("dp")
    z = lax.axis_index("expert")
    y, x, core = dp // 4, lax.rem(dp // 2, 2), lax.rem(dp, 2)
    core_peer, x_peer, y_peer = dp + 1 - 2 * core, dp + 2 - 4 * x, dp + 4 - 8 * y

    def loads(e, slot):
        return (
            pltpu.make_async_copy(
                gated_hbm.at[:, pl.ds(pl.multiple_of(e * ff_width, ff_width), ff_width)],
                gated.at[slot],
                load_sem.at[slot, 0],
            ),
            pltpu.make_async_copy(
                inner_hbm.at[:, pl.ds(pl.multiple_of(2 * e * ff_width, ff_width), 2 * ff_width)],
                inner.at[slot],
                load_sem.at[slot, 1],
            ),
        )

    row_load = pltpu.make_async_copy(rows_hbm, rows, load_sem.at[0, 2])
    cot_load = pltpu.make_async_copy(cots_hbm, cots, load_sem.at[1, 2])
    row_load.start()
    for copy in loads(0, 0):
        copy.start()
    cot_load.start()
    barrier = pltpu.get_barrier_semaphore()
    for peer in (core_peer, x_peer, y_peer):
        pl.semaphore_signal(barrier, inc=1, device_id=(peer, z), device_id_type=MESH)
    pl.semaphore_wait(barrier, 3)
    row_load.wait()
    cot_load.wait()

    def send(stage, e, source, target, peer):
        return pltpu.make_async_remote_copy(
            src_ref=source,
            dst_ref=target,
            send_sem=send_sem.at[stage, e],
            recv_sem=recv_sem.at[stage, e],
            device_id=(peer, z),
            device_id_type=MESH,
        )

    def core_send(e):
        return send(0, e, grads.at[e, :, :, 1 - core], core_sum.at[e], core_peer)

    def first_send(e, along_x):
        if along_x:
            return send(1, e, core_sum.at[e, :, 1 - x], first_sum.at[e], x_peer)
        return send(1, e, core_sum.at[e, 1 - y], first_sum.at[e], y_peer)

    def last_send(e, along_x):
        if along_x:
            return send(2, e, first_sum.at[e, 1 - x], last_sum.at[e], x_peer)
        return send(2, e, first_sum.at[e, 1 - y], last_sum.at[e], y_peer)

    def by_parity(e, act):
        even = lax.rem(e, 2) == 0

        @pl.when(even)
        def _():
            act(True)

        @pl.when(jnp.logical_not(even))
        def _():
            act(False)

    def after_core(e):
        core_send(e).wait_recv()
        for yy in range(2):
            for xx in range(2):
                core_sum[e, yy, xx] = (
                    grads[e, yy, xx, core].astype(F32) + core_sum[e, yy, xx].astype(F32)
                ).astype(BF16)
        by_parity(e, lambda even: first_send(e, even).start())

    def after_first(e):
        def act(even):
            first_send(e, even).wait_recv()
            for other in range(2):
                kept = core_sum[e, other, x] if even else core_sum[e, y, other]
                first_sum[e, other] = (
                    kept.astype(F32) + first_sum[e, other].astype(F32)
                ).astype(BF16)
            last_send(e, not even).start()

        by_parity(e, act)

    def after_last(e):
        def act(even):
            last_send(e, not even).wait_recv()
            kept = first_sum[e, y] if even else first_sum[e, x]
            total[e] = kept.astype(F32) + last_sum[e].astype(F32)

        by_parity(e, act)
        pltpu.make_async_copy(total.at[e], sum_hbm.at[e], out_sem.at[e]).start()

    def step(e, _):
        slot = lax.rem(e, 2)
        for copy in loads(e, slot):
            copy.wait()

        @pl.when(e + 1 < experts)
        def _():
            for copy in loads(e + 1, 1 - slot):
                copy.start()

        def tile(at, _):
            columns = pl.ds(pl.multiple_of(at * 2 * block_rows, 2 * block_rows), 2 * block_rows)
            up_grad = contract(rows[:, columns], inner[slot], 0, 0).astype(BF16)
            down_grad = contract(cots[:, columns], gated[slot], 0, 0).astype(BF16)
            for side in range(2):
                part = slice(side * block_rows, (side + 1) * block_rows)
                grads[e, at // 2, lax.rem(at, 2), side, :, : 2 * ff_width] = up_grad[part]
                grads[e, at // 2, lax.rem(at, 2), side, :, 2 * ff_width :] = down_grad[part]
            return 0

        lax.fori_loop(0, 4, tile, 0)
        core_send(e).start()

        @pl.when(e >= 1)
        def _():
            after_core(e - 1)

        @pl.when(e >= 3)
        def _():
            after_first(e - 3)

        return 0

    lax.fori_loop(0, experts, step, 0)
    after_core(experts - 1)

    for e in range(max(experts - 3, 0), experts):
        after_first(e)
        if e - 2 >= 0:
            after_last(e - 2)
    for e in range(max(experts - 2, 0), experts):
        after_last(e)
    for e in range(experts):
        core_send(e).wait_send()
        first_send(e, e % 2 == 0).wait_send()
        last_send(e, e % 2 == 1).wait_send()
        pltpu.make_async_copy(total.at[e], sum_hbm.at[e], out_sem.at[e]).wait()


def bank_grads(rows, cots, gated, inner, experts):
    tokens, width = rows.shape
    ff_width = gated.shape[1] // experts
    lanes = 3 * ff_width
    block_rows = width // 8
    anywhere = pl.BlockSpec(memory_space=pl.ANY)
    return pl.pallas_call(
        bank_grads_kernel,
        out_shape=jax.ShapeDtypeStruct((experts, block_rows, lanes), F32),
        in_specs=[anywhere] * 4,
        out_specs=anywhere,
        scratch_shapes=[
            pltpu.VMEM((tokens, width), BF16),
            pltpu.VMEM((tokens, width), BF16),
            pltpu.VMEM((2, tokens, ff_width), BF16),
            pltpu.VMEM((2, tokens, 2 * ff_width), BF16),
            pltpu.VMEM((experts, 2, 2, 2, block_rows, lanes), BF16),
            pltpu.VMEM((experts, 2, 2, block_rows, lanes), BF16),
            pltpu.VMEM((experts, 2, block_rows, lanes), BF16),
            pltpu.VMEM((experts, block_rows, lanes), BF16),
            pltpu.VMEM((experts, block_rows, lanes), F32),
            pltpu.SemaphoreType.DMA((2, 3)),
            pltpu.SemaphoreType.DMA((3, experts)),
            pltpu.SemaphoreType.DMA((3, experts)),
            pltpu.SemaphoreType.DMA((experts,)),
        ],
        compiler_params=pltpu.CompilerParams(
            collective_id=2, has_side_effects=True, vmem_limit_bytes=VMEM_MOST
        ),
        cost_estimate=pl.CostEstimate(
            flops=6 * tokens * width * experts * ff_width,
            bytes_accessed=2**27,
            transcendentals=0,
        ),
    )(rows, cots, gated, inner)


PAIR = 2 * HEAD_DIM
UNIT = 512


def line_gather(line, z, dp, source, landing, send_sem, recv_sem):
    def copy(origin, block, sem, target):
        return pltpu.make_async_remote_copy(
            src_ref=origin,
            dst_ref=landing.at[block],
            send_sem=send_sem.at[sem],
            recv_sem=recv_sem.at[block],
            device_id=(dp, target),
            device_id_type=MESH,
        )

    def start():
        @pl.when(z < line - 1)
        def _():
            copy(source, z, line, z + 1).start()

        @pl.when(z > 0)
        def _():
            copy(source, z, line + 1, z - 1).start()

    def pass_on(apart):
        low = jnp.maximum(z - apart, 0)
        high = jnp.minimum(z + apart, line - 1)

        @pl.when(z - apart >= 0)
        def _():
            copy(source, low, low, z).wait_recv()

            @pl.when(z < line - 1)
            def _():
                copy(landing.at[low], low, low, z + 1).start()

        @pl.when(z + apart < line)
        def _():
            copy(source, high, high, z).wait_recv()

            @pl.when(z > 0)
            def _():
                copy(landing.at[high], high, high, z - 1).start()

    def finish():
        @pl.when(z < line - 1)
        def _():
            copy(source, z, line, z + 1).wait_send()

        @pl.when(z > 0)
        def _():
            copy(source, z, line + 1, z - 1).wait_send()

        for s in range(line):

            @pl.when(((s < z) & (z < line - 1)) | ((s > z) & (z > 0)))
            def _(s=s):
                copy(source, s, s, z).wait_send()

    return start, pass_on, finish


def swap_halves(value):
    lane = lax.broadcasted_iota(jnp.int32, value.shape, 1)
    half = HEAD_DIM // 2
    return jnp.where(
        lax.rem(lane, HEAD_DIM) < half,
        pltpu.roll(value, value.shape[1] - half, 1),
        pltpu.roll(value, half, 1),
    )


def sides(pair, side, scale):
    value = pair.astype(F32)
    if scale is not None:
        value = value * scale
    turned = pltpu.roll(value, HEAD_DIM, 1)
    lane = lax.broadcasted_iota(jnp.int32, value.shape, 1)
    left, right = (value, turned) if side == 0 else (turned, value)
    return (
        jnp.where(lane < HEAD_DIM, left, 0.0).astype(BF16),
        jnp.where(lane < HEAD_DIM, 0.0, right).astype(BF16),
    )


def lanes_at(start, size):
    return pl.ds(pl.multiple_of(start, 128), size)


def attend_kernel(
    line,
    tokens,
    cots_hbm,
    gain_rows,
    heads_in,
    heads_out,
    router_rows,
    route_rows,
    cosine,
    sine,
    bias,
    first_in,
    queries,
    keys,
    values,
    attended,
    hidden,
    second_in,
    gate_rows,
    log_totals,
    cots_all,
    send_sem,
    recv_sem,
    own_sem,
):
    dp = lax.axis_index("dp")
    z = lax.axis_index("expert")
    start, pass_on, finish = line_gather(line, z, dp, cots_hbm, cots_all, send_sem, recv_sem)
    barrier = pltpu.get_barrier_semaphore()
    for step in range(1, line):
        pl.semaphore_signal(
            barrier, inc=1, device_id=(dp, lax.rem(z + step, line)), device_id_type=MESH
        )
    pl.semaphore_wait(barrier, line - 1)
    start()
    own = pltpu.make_async_copy(cots_hbm, cots_all.at[z], own_sem)
    own.start()

    query_end = HEADS * HEAD_DIM
    key_end = query_end + KV_HEADS * HEAD_DIM
    token_rows = tokens[...].astype(F32)
    factor = lax.rsqrt(jnp.mean(token_rows * token_rows, axis=1, keepdims=True) + EPS)
    first_in[...] = (token_rows * factor * gain_rows[0:1]).astype(BF16)
    log_totals[...] = jnp.zeros_like(log_totals)

    def pair(j, _):
        for side in range(2):
            wide = contract(
                first_in[...], heads_in[:, lanes_at((2 * j + side) * PAIR, PAIR)], 1, 0
            )
            queries[:, lanes_at((2 * j + side) * PAIR, PAIR)] = (
                wide * cosine[...] + swap_halves(wide) * sine[...]
            ).astype(BF16)
        wide = contract(first_in[...], heads_in[:, lanes_at(query_end + j * PAIR, PAIR)], 1, 0)
        keys[:, lanes_at(j * PAIR, PAIR)] = (
            wide * cosine[...] + swap_halves(wide) * sine[...]
        ).astype(BF16)
        values[:, lanes_at(j * PAIR, PAIR)] = contract(
            first_in[...], heads_in[:, lanes_at(key_end + j * PAIR, PAIR)], 1, 0
        ).astype(BF16)
        for side in range(2):
            group = queries[:, lanes_at((2 * j + side) * PAIR, PAIR)]
            key_sides = sides(keys[:, lanes_at(j * PAIR, PAIR)], side, SCALE)
            value_sides = sides(values[:, lanes_at(j * PAIR, PAIR)], side, None)
            total = jnp.zeros(group.shape, F32)
            for member in range(2):
                scores = contract(group, key_sides[member], 1, 1) + bias[...]
                peak = jnp.max(scores, axis=1, keepdims=True)
                powers = jnp.exp(scores - peak)
                amount = jnp.sum(powers, axis=1, keepdims=True)
                lane = lax.broadcasted_iota(jnp.int32, log_totals.shape, 1)
                log_totals[...] = jnp.where(
                    lane == 4 * j + 2 * side + member, peak + jnp.log(amount), log_totals[...]
                )
                weights = (powers * (1.0 / amount)).astype(BF16)
                total = total + contract(weights, value_sides[member], 1, 0)
            attended[:, lanes_at((2 * j + side) * PAIR, PAIR)] = total.astype(BF16)
        return 0

    lax.fori_loop(0, KV_HEADS // 2, pair, 0)
    pass_on(1)
    hidden_rows = token_rows + contract(attended[...], heads_out[...], 1, 1)
    hidden[...] = hidden_rows
    factor = lax.rsqrt(jnp.mean(hidden_rows * hidden_rows, axis=1, keepdims=True) + EPS)
    second = (hidden_rows * factor * gain_rows[1:2]).astype(BF16)
    second_in[...] = second
    logits = contract(router_rows[...], second, 1, 1)
    expert = lax.broadcasted_iota(jnp.int32, logits.shape, 0)
    named = expert == route_rows[0:1]
    for k in range(1, route_rows.shape[0]):
        named = named | (expert == route_rows[k : k + 1])
    peak = jnp.max(jnp.where(named, logits, -1e30), axis=0, keepdims=True)
    powers = jnp.where(named, jnp.exp(jnp.where(named, logits, peak) - peak), 0.0)
    gate_rows[...] = powers / jnp.sum(powers, axis=0, keepdims=True)
    for apart in range(2, line):
        pass_on(apart)
    finish()
    own.wait()


def attend(tokens, cots, gain_rows, heads_in, heads_out, router_rows, route_rows, tables, line):
    count, width = tokens.shape
    experts = router_rows.shape[0]
    kv_width = KV_HEADS * HEAD_DIM
    shape = jax.ShapeDtypeStruct
    held = pl.BlockSpec(memory_space=pltpu.VMEM)
    anywhere = pl.BlockSpec(memory_space=pl.ANY)
    return pl.pallas_call(
        functools.partial(attend_kernel, line),
        out_shape=(
            shape((count, width), BF16),
            shape((count, HEADS * HEAD_DIM), BF16),
            shape((count, kv_width), BF16),
            shape((count, kv_width), BF16),
            shape((count, HEADS * HEAD_DIM), BF16),
            shape((count, width), F32),
            shape((count, width), BF16),
            shape((experts, count), F32),
            shape((count, 128), F32),
            shape((line, count, width), BF16),
        ),
        in_specs=[held, anywhere] + [held] * 8,
        out_specs=(held,) * 9 + (anywhere,),
        scratch_shapes=[
            pltpu.SemaphoreType.DMA((line + 2,)),
            pltpu.SemaphoreType.DMA((line,)),
            pltpu.SemaphoreType.DMA,
        ],
        compiler_params=pltpu.CompilerParams(
            collective_id=4, has_side_effects=True, vmem_limit_bytes=VMEM_MOST
        ),
        cost_estimate=pl.CostEstimate(flops=2**33, bytes_accessed=2**24, transcendentals=2**21),
    )(tokens, cots, gain_rows, heads_in, heads_out, router_rows, route_rows, *tables)


def attend_back_kernel(
    paired,
    line,
    back_rows,
    hidden,
    cots,
    second_in,
    gate_rows,
    gate_grads,
    router_rows,
    gain_rows,
    heads_out,
    queries,
    keys,
    values,
    attended,
    log_totals,
    cosine,
    sine,
    bias,
    tokens_hbm,
    first_hbm,
    in_hbm,
    token_grad,
    sum_hbm,
    small_hbm,
    tokens,
    first_in,
    heads_in,
    grad_hidden,
    grad_attended,
    grad_projected,
    small_rows,
    own,
    own_small,
    *scratch,
):
    dp = lax.axis_index("dp")
    z = lax.axis_index("expert")
    units = own.shape[0]
    block_rows = own.shape[4]
    load_sem = scratch[0]
    loads = (
        pltpu.make_async_copy(first_hbm, first_in, load_sem.at[0]),
        pltpu.make_async_copy(tokens_hbm, tokens, load_sem.at[1]),
        pltpu.make_async_copy(in_hbm, heads_in, load_sem.at[2]),
    )
    for copy in loads:
        copy.start()
    if paired:
        (
            cores,
            firsts,
            lasts,
            sums,
            lines,
            totals,
            small_cores,
            small_firsts,
            small_lasts,
            small_sums,
            small_lines,
            small_totals,
            send_sem,
            recv_sem,
            line_send,
            line_recv,
            out_sem,
        ) = scratch[1:]
        rows = totals.shape[1]
        y, x, core = dp // 4, lax.rem(dp // 2, 2), lax.rem(dp, 2)
        core_peer, x_peer, y_peer = dp + 1 - 2 * core, dp + 2 - 4 * x, dp + 4 - 8 * y
        barrier = pltpu.get_barrier_semaphore()
        for peer in (core_peer, x_peer, y_peer):
            pl.semaphore_signal(barrier, inc=1, device_id=(peer, z), device_id_type=MESH)
        for step in range(1, line):
            pl.semaphore_signal(
                barrier, inc=1, device_id=(dp, lax.rem(z + step, line)), device_id_type=MESH
            )
        pl.semaphore_wait(barrier, 3 + line - 1)
        buffers = (own, cores, firsts, lasts, sums, lines, totals)
        small_buffers = (
            own_small,
            small_cores,
            small_firsts,
            small_lasts,
            small_sums,
            small_lines,
            small_totals,
        )

        def send(stage, u, source, target, peer):
            return pltpu.make_async_remote_copy(
                src_ref=source,
                dst_ref=target,
                send_sem=send_sem.at[stage, u],
                recv_sem=recv_sem.at[stage, u],
                device_id=(peer, z),
                device_id_type=MESH,
            )

        class Sums:
            def __init__(self, held, shift):
                self.own, self.cores, self.firsts, self.lasts = held[:4]
                self.sums, self.lines, self.totals = held[4:]
                self.shift = shift

            def core_send(self, u):
                return send(
                    0,
                    u + self.shift,
                    self.own.at[u, :, :, 1 - core],
                    self.cores.at[u],
                    core_peer,
                )

            def first_send(self, u, along_x):
                if along_x:
                    source, peer = self.cores.at[u, :, 1 - x], x_peer
                else:
                    source, peer = self.cores.at[u, 1 - y], y_peer
                return send(1, u + self.shift, source, self.firsts.at[u], peer)

            def last_send(self, u, along_x):
                if along_x:
                    source, peer = self.firsts.at[u, 1 - x], x_peer
                else:
                    source, peer = self.firsts.at[u, 1 - y], y_peer
                return send(2, u + self.shift, source, self.lasts.at[u], peer)

            def line_copy(self, u, step):
                peer = lax.rem(z + step, line)
                return pltpu.make_async_remote_copy(
                    src_ref=self.sums.at[u, pl.ds(pl.multiple_of(peer * rows, rows), rows)],
                    dst_ref=self.lines.at[u, step],
                    send_sem=line_send.at[u + self.shift, step],
                    recv_sem=line_recv.at[u + self.shift, step],
                    device_id=(dp, peer),
                    device_id_type=MESH,
                )

            def by_parity(self, u, act):
                even = lax.rem(jnp.int32(u), 2) == 0

                @pl.when(even)
                def _():
                    act(True)

                @pl.when(jnp.logical_not(even))
                def _():
                    act(False)

            def after_core(self, u):
                self.core_send(u).wait_recv()
                for yy in range(2):
                    for xx in range(2):
                        self.cores[u, yy, xx] = (
                            self.own[u, yy, xx, core].astype(F32)
                            + self.cores[u, yy, xx].astype(F32)
                        ).astype(BF16)
                self.by_parity(u, lambda even: self.first_send(u, even).start())

            def after_first(self, u):
                def act(even):
                    self.first_send(u, even).wait_recv()
                    for other in range(2):
                        kept = self.cores[u, other, x] if even else self.cores[u, y, other]
                        self.firsts[u, other] = (
                            kept.astype(F32) + self.firsts[u, other].astype(F32)
                        ).astype(BF16)
                    self.last_send(u, not even).start()

                self.by_parity(u, act)

            def after_last(self, u):
                def act(even):
                    self.last_send(u, not even).wait_recv()
                    kept = self.firsts[u, y] if even else self.firsts[u, x]
                    self.sums[u] = (kept.astype(F32) + self.lasts[u].astype(F32)).astype(BF16)

                self.by_parity(u, act)
                for step in range(1, line):
                    self.line_copy(u, step).start()

            def after_line(self, u):
                value = self.sums[u, pl.ds(pl.multiple_of(z * rows, rows), rows)].astype(F32)
                for step in range(1, line):
                    self.line_copy(u, step).wait_recv()
                    value = value + self.lines[u, step].astype(F32)
                self.totals[u] = value

            def finish(self, u):
                self.core_send(u).wait_send()
                self.first_send(u, u % 2 == 0).wait_send()
                self.last_send(u, u % 2 == 1).wait_send()
                for step in range(1, line):
                    self.line_copy(u, step).wait_send()

        wide_sums = Sums(buffers, 0)
        small_sum = Sums(small_buffers, units)

    def keep(target, u, value):
        for block in range(8):
            target[u, block // 4, block // 2 % 2, block % 2] = value[
                block * block_rows : (block + 1) * block_rows
            ]

    gates = gate_rows[...]
    gate_grad = gate_grads[...]
    logit_grad = gates * (gate_grad - jnp.sum(gates * gate_grad, axis=0, keepdims=True))
    high = logit_grad.astype(BF16)
    low = (logit_grad - high.astype(F32)).astype(BF16)
    grad_second = (
        back_rows[...].astype(F32)
        + contract(high, router_rows[...], 0, 0)
        + contract(low, router_rows[...], 0, 0)
    )
    small_rows[...] = jnp.zeros_like(small_rows)
    experts = high.shape[0]
    small_rows[:experts] = contract(high, second_in[...], 1, 0) + contract(low, second_in[...], 1, 0)

    def norm_back(incoming, rows, gain):
        factor = lax.rsqrt(jnp.mean(rows * rows, axis=1, keepdims=True) + EPS)
        normed = rows * factor
        gain_grad = jnp.sum(incoming * normed, axis=0, keepdims=True)
        weighted = incoming * gain
        mean = jnp.mean(weighted * normed, axis=1, keepdims=True)
        return factor * (weighted - normed * mean), gain_grad

    norm_grad, gain_grad = norm_back(grad_second, hidden[...], gain_rows[1:2])
    small_rows[experts + 1 : experts + 2] = gain_grad
    grad_hidden[...] = cots[...].astype(F32) + norm_grad
    branch = grad_hidden[...].astype(BF16)
    for u in range(2):
        keep(
            own,
            u,
            contract(branch, attended[:, u * UNIT : (u + 1) * UNIT], 0, 0).astype(BF16),
        )
        if paired:
            wide_sums.core_send(u).start()
    grad_attended[...] = contract(branch, heads_out[...], 1, 0).astype(BF16)
    loads[0].wait()
    if paired:
        wide_sums.after_core(0)

    def pair(j, _):
        key_pair = keys[:, lanes_at(j * PAIR, PAIR)]
        value_pair = values[:, lanes_at(j * PAIR, PAIR)]
        key_grads = []
        value_grads = []
        for side in range(2):
            at = lanes_at((2 * j + side) * PAIR, PAIR)
            group = queries[:, at]
            group_grad = grad_attended[:, at]
            key_sides = sides(key_pair, side, SCALE)
            value_sides = sides(value_pair, side, None)
            product = group_grad.astype(F32) * attended[:, at].astype(F32)
            lane = lax.broadcasted_iota(jnp.int32, product.shape, 1)
            grad = jnp.zeros(group.shape, F32)
            key_grad = []
            value_grad = []
            for member in range(2):
                head = 4 * j + 2 * side + member
                log_total = jnp.sum(
                    jnp.where(lane == head, log_totals[...], 0.0), axis=1, keepdims=True
                )
                mine = (lane < HEAD_DIM) if member == 0 else (lane >= HEAD_DIM)
                spread = jnp.sum(jnp.where(mine, product, 0.0), axis=1, keepdims=True)
                scores = contract(group, key_sides[member], 1, 1) + bias[...]
                weights = jnp.exp(scores - log_total)
                weight_grads = contract(group_grad, value_sides[member], 1, 1)
                score_grads = (weights * (weight_grads - spread)).astype(BF16)
                grad = grad + contract(score_grads, key_sides[member], 1, 0)
                rows_of = slice(member * HEAD_DIM, (member + 1) * HEAD_DIM)
                key_grad.append(contract(group, score_grads, 0, 0)[rows_of])
                value_grad.append(contract(group_grad, weights.astype(BF16), 0, 0)[rows_of])
            grad_projected[j, :, side * PAIR : (side + 1) * PAIR] = (
                grad * cosine[...] - swap_halves(grad) * sine[...]
            ).astype(BF16)
            key_grads.append(key_grad[0] + key_grad[1])
            value_grads.append(value_grad[0] + value_grad[1])
        key_rows = jnp.concatenate(key_grads, axis=0).T * SCALE
        grad_projected[j, :, 2 * PAIR : 3 * PAIR] = (
            key_rows * cosine[...] - swap_halves(key_rows) * sine[...]
        ).astype(BF16)
        grad_projected[j, :, 3 * PAIR :] = jnp.concatenate(value_grads, axis=0).T.astype(BF16)
        keep(own, 2 + j, contract(first_in[...], grad_projected[j], 0, 0).astype(BF16))
        if paired:
            wide_sums.core_send(2 + j).start()
            wide_sums.after_core(1 + j)
            wide_sums.after_first(j)

            @pl.when(j >= 1)
            def _():
                wide_sums.after_last(j - 1)

            @pl.when(j >= 2)
            def _():
                wide_sums.after_line(j - 2)

        return 0

    pairs = KV_HEADS // 2
    lax.fori_loop(0, pairs, pair, 0)
    last = units - 1
    if paired:
        wide_sums.after_core(last)
        wide_sums.after_first(last - 1)
        wide_sums.after_last(last - 2)
    loads[1].wait()
    loads[2].wait()
    grad_first = jnp.zeros(grad_hidden.shape, F32)
    query_end = HEADS * HEAD_DIM
    key_end = query_end + KV_HEADS * HEAD_DIM
    for j in range(pairs):
        for at, begin, size in (
            (0, 2 * j * PAIR, 2 * PAIR),
            (2 * PAIR, query_end + j * PAIR, PAIR),
            (3 * PAIR, key_end + j * PAIR, PAIR),
        ):
            grad_first = grad_first + contract(
                grad_projected[j, :, at : at + size], heads_in[:, begin : begin + size], 1, 1
            )
    norm_grad, gain_grad = norm_back(grad_first, tokens[...].astype(F32), gain_rows[0:1])
    small_rows[experts : experts + 1] = gain_grad
    keep(own_small, 0, small_rows[...].T.astype(BF16))
    if paired:
        small_sum.core_send(0).start()
    token_grad[...] = grad_hidden[...] + norm_grad
    if paired:
        wide_sums.after_line(last - 3)
        small_sum.after_core(0)
        wide_sums.after_first(last)
        wide_sums.after_last(last - 1)
        wide_sums.after_line(last - 2)
        small_sum.after_first(0)
        wide_sums.after_last(last)
        small_sum.after_last(0)
        wide_sums.after_line(last - 1)
        wide_sums.after_line(last)
        small_sum.after_line(0)
        outs = (
            pltpu.make_async_copy(totals, sum_hbm, out_sem.at[0]),
            pltpu.make_async_copy(small_totals, small_hbm, out_sem.at[1]),
        )
    else:
        outs = (
            pltpu.make_async_copy(own, sum_hbm, load_sem.at[3]),
            pltpu.make_async_copy(own_small, small_hbm, load_sem.at[4]),
        )
    for copy in outs:
        copy.start()
    if paired:
        for u in range(units):
            wide_sums.finish(u)
        small_sum.finish(0)
    for copy in outs:
        copy.wait()


def attend_back(held_args, far_args, paired, line):
    tokens, first_in, heads_in = far_args
    count, width = tokens.shape
    pairs = KV_HEADS // 2
    units = 2 + pairs
    block_rows = width // 8
    rows = block_rows // line
    shape = jax.ShapeDtypeStruct
    held = pl.BlockSpec(memory_space=pltpu.VMEM)
    anywhere = pl.BlockSpec(memory_space=pl.ANY)
    if paired:
        sum_shapes = (shape((units, rows, UNIT), F32), shape((1, rows, 128), F32))
    else:
        sum_shapes = (
            shape((units, 2, 2, 2, block_rows, UNIT), BF16),
            shape((1, 2, 2, 2, block_rows, 128), BF16),
        )
    exchange = []
    if paired:
        for number, lanes in ((units, UNIT), (1, 128)):
            exchange += [
                pltpu.VMEM((number, 2, 2, block_rows, lanes), BF16),
                pltpu.VMEM((number, 2, block_rows, lanes), BF16),
                pltpu.VMEM((number, block_rows, lanes), BF16),
                pltpu.VMEM((number, block_rows, lanes), BF16),
                pltpu.VMEM((number, line, rows, lanes), BF16),
                pltpu.VMEM((number, rows, lanes), F32),
            ]
        exchange += [
            pltpu.SemaphoreType.DMA((3, units + 1)),
            pltpu.SemaphoreType.DMA((3, units + 1)),
            pltpu.SemaphoreType.DMA((units + 1, line)),
            pltpu.SemaphoreType.DMA((units + 1, line)),
            pltpu.SemaphoreType.DMA((2,)),
        ]
    settings = dict(vmem_limit_bytes=VMEM_MOST)
    if paired:
        settings.update(collective_id=3, has_side_effects=True)
    return pl.pallas_call(
        functools.partial(attend_back_kernel, paired, line),
        out_shape=(shape((count, width), F32),) + sum_shapes,
        in_specs=[held] * len(held_args) + [anywhere] * 3,
        out_specs=(held, anywhere, anywhere),
        scratch_shapes=[
            pltpu.VMEM((count, width), BF16),
            pltpu.VMEM((count, width), BF16),
            pltpu.VMEM(heads_in.shape, BF16),
            pltpu.VMEM((count, width), F32),
            pltpu.VMEM((count, HEADS * HEAD_DIM), BF16),
            pltpu.VMEM((pairs, count, 4 * PAIR), BF16),
            pltpu.VMEM((128, width), F32),
            pltpu.VMEM((units, 2, 2, 2, block_rows, UNIT), BF16),
            pltpu.VMEM((1, 2, 2, 2, block_rows, 128), BF16),
            pltpu.SemaphoreType.DMA((5,)),
            *exchange,
        ],
        compiler_params=pltpu.CompilerParams(**settings),
        cost_estimate=pl.CostEstimate(flops=2**34, bytes_accessed=2**25, transcendentals=2**21),
    )(*held_args, *far_args)


def unit_columns(sums):
    pairs = KV_HEADS // 2
    parts = sums[2 : 2 + pairs]
    rows = sums.shape[1]

    def side_by_side(value):
        return jnp.transpose(value, (1, 0, 2)).reshape(rows, -1)

    return (
        jnp.concatenate(
            [
                side_by_side(parts[:, :, : 2 * PAIR]),
                side_by_side(parts[:, :, 2 * PAIR : 3 * PAIR]),
                side_by_side(parts[:, :, 3 * PAIR :]),
            ],
            axis=1,
        ),
        side_by_side(sums[:2]),
    )


def body(
    tokens,
    cotangent,
    routes,
    cont_ids,
    norm_gains,
    gains_moment,
    gains_average,
    heads_in,
    heads_in_master,
    heads_in_moment,
    heads_in_average,
    heads_out,
    heads_out_master,
    heads_out_moment,
    heads_out_average,
    router,
    router_master,
    router_moment,
    router_average,
    expert_in,
    expert_in_master,
    expert_in_moment,
    expert_in_average,
    expert_out,
    expert_out_master,
    expert_out_moment,
    expert_out_average,
):
    token_count, model_width = tokens.shape
    local_experts = expert_in.shape[0]
    peer_count = lax.axis_size("expert")
    experts = local_experts * peer_count
    paired = lax.axis_size("dp") == 8 and peer_count == 4
    positions, allowed = layout(cont_ids[0], token_count - cont_ids.shape[1])
    tables = (*rope_tables(positions), jnp.where(allowed, 0.0, -1e30))
    gain_rows = norm_gains.T
    router_rows = router.T
    (
        first_in,
        queries,
        key_rows,
        value_rows,
        attended,
        hidden,
        second_in,
        gates,
        log_totals,
        cots_all,
    ) = attend(
        tokens,
        cotangent,
        gain_rows,
        heads_in,
        heads_out,
        router_rows,
        routes.T,
        tables,
        peer_count,
    )
    padded = -local_experts % 8
    gate_rows = jnp.pad(
        gates.reshape(peer_count, local_experts, token_count), ((0, 0), (0, padded), (0, 0))
    )
    mix_part, grad_part, gate_grads, gated, grad_gate_up, rows_all = bank(
        second_in, cots_all, gate_rows, expert_in, expert_out, peer_count
    )
    back_rows = lax.psum_scatter(
        grad_part.reshape(peer_count * token_count, model_width),
        "expert",
        scatter_dimension=0,
        tiled=True,
    )
    grad_sources = (
        rows_all.reshape(peer_count * token_count, model_width),
        cots_all.reshape(peer_count * token_count, model_width),
        gated.reshape(peer_count * token_count, -1),
        grad_gate_up.reshape(peer_count * token_count, -1),
    )
    if paired:
        bank_sums = bank_grads(*grad_sources, local_experts)
        expert_sums = (bank_sums[:, :, : expert_in.shape[2]], bank_sums[:, :, expert_in.shape[2] :])
    else:
        expert_sums = tuple(
            lax.psum_scatter(part, "dp", scatter_dimension=1, tiled=True).astype(jnp.float32)
            for part in weight_grads(*grad_sources, local_experts)
        )
    mix_part, back_rows, expert_sums = lax.optimization_barrier(
        (mix_part, back_rows, expert_sums)
    )
    mixture = lax.psum_scatter(
        mix_part.reshape(peer_count * token_count, model_width),
        "expert",
        scatter_dimension=0,
        tiled=True,
    ).astype(jnp.float32)
    output = (hidden + mixture).astype(jnp.bfloat16)
    token_grad, unit_sums, small_sum = attend_back(
        (
            back_rows,
            hidden,
            cotangent,
            second_in,
            gates,
            gate_grads[:, :local_experts].reshape(experts, token_count),
            router_rows,
            gain_rows,
            heads_out,
            queries,
            key_rows,
            value_rows,
            attended,
            log_totals,
            *tables,
        ),
        (tokens, first_in, heads_in),
        paired,
        peer_count,
    )
    if paired:
        small_sum = small_sum[0]
    else:
        head_parts = unit_columns(unit_sums.reshape(unit_sums.shape[0], model_width, UNIT))
        packed = jnp.concatenate([*head_parts, small_sum.reshape(model_width, 128)], axis=1)
        head_total = lax.psum_scatter(
            packed, ("dp", "expert"), scatter_dimension=0, tiled=True
        ).astype(jnp.float32)
        cut_in = head_parts[0].shape[1]
        cut_out = cut_in + head_parts[1].shape[1]
        head_parts = (head_total[:, :cut_in], head_total[:, cut_in:cut_out])
        small_sum = head_total[:, cut_out:]
    if paired:
        head_parts = unit_columns(unit_sums)
    head_in_sum, head_out_sum = head_parts
    summed = (
        head_in_sum,
        head_out_sum,
        small_sum[:, :experts],
        small_sum[:, experts : experts + 2],
    )
    shard_rows = model_width // lax.axis_size(("dp", "expert"))
    gains_share = lax.dynamic_slice_in_dim(
        norm_gains, lax.axis_index(("dp", "expert")) * shard_rows, shard_rows, 0
    )
    gains_new = update(summed[3], gains_share, gains_moment, gains_average)
    inproj_new = update(summed[0], heads_in_master, heads_in_moment, heads_in_average)
    outproj_new = update(summed[1], heads_out_master, heads_out_moment, heads_out_average)
    router_new = update(summed[2], router_master, router_moment, router_average)
    upper_new = update(expert_sums[0], expert_in_master, expert_in_moment, expert_in_average)
    lower_new = update(expert_sums[1], expert_out_master, expert_out_moment, expert_out_average)
    return (
        output,
        token_grad,
        gains_new[0],
        gains_new[1],
        gains_new[2],
        inproj_new[0],
        inproj_new[1],
        inproj_new[2],
        outproj_new[0],
        outproj_new[1],
        outproj_new[2],
        router_new[0],
        router_new[1],
        router_new[2],
        upper_new[0],
        upper_new[1],
        upper_new[2],
        lower_new[0],
        lower_new[1],
        lower_new[2],
    )


def solution(mesh):
    return jax.shard_map(
        body,
        mesh=mesh,
        in_specs=(
            P(("dp", "expert"), None),
            P(("dp", "expert"), None),
            P(("dp", "expert"), None),
            P(("dp", "expert"), None),
            P(),
            P(("dp", "expert"), None),
            P(("dp", "expert"), None),
            P(),
            P(("dp", "expert"), None),
            P(("dp", "expert"), None),
            P(("dp", "expert"), None),
            P(),
            P(("dp", "expert"), None),
            P(("dp", "expert"), None),
            P(("dp", "expert"), None),
            P(),
            P(("dp", "expert"), None),
            P(("dp", "expert"), None),
            P(("dp", "expert"), None),
            P("expert", None, None),
            P("expert", "dp", None),
            P("expert", "dp", None),
            P("expert", "dp", None),
            P("expert", None, None),
            P("expert", "dp", None),
            P("expert", "dp", None),
            P("expert", "dp", None),
        ),
        out_specs=(
            P(("dp", "expert"), None),
            P(("dp", "expert"), None),
            P(("dp", "expert"), None),
            P(("dp", "expert"), None),
            P(("dp", "expert"), None),
            P(("dp", "expert"), None),
            P(("dp", "expert"), None),
            P(("dp", "expert"), None),
            P(("dp", "expert"), None),
            P(("dp", "expert"), None),
            P(("dp", "expert"), None),
            P(("dp", "expert"), None),
            P(("dp", "expert"), None),
            P(("dp", "expert"), None),
            P("expert", "dp", None),
            P("expert", "dp", None),
            P("expert", "dp", None),
            P("expert", "dp", None),
            P("expert", "dp", None),
            P("expert", "dp", None),
        ),
        check_vma=False,
    )
```

profile of v0, /device:TPU:0, one launch (start us, length us, event | category | flops | bytes accessed | tf_op | source)
XLA Modules:
  0.0 348.1 jit_solution(15523382958463788218)
XLA Ops:
  7.2 0.0 reduce-scatter.3.cloned.1.call-start
  7.3 0.9 convert_reduce_fusion
  8.2 0.7 concatenate.22
  8.9 0.8 fusion.2
  9.6 1.0 fusion.1.bias
  10.6 1.1 pad_maximum_fusion
  11.7 64.3 %shard_map.410 = (bf16[384,1024]{1,0:T(8,128)(2,1)}, bf16[384,1024]{1,0:T(8,128)(2,1)}, bf16[384,512]{1,0:T(8,128)(2,1)}, bf16[384,512]{1,0:T(8,128)(2,1)}, bf16...) custom-call(bf16[384,1024]{1,0:T(8,128)(2,1)} %tokens_hbm.1, ...), custom_call_target="tpu_custom_call" | custom-call | flops 8589934592 | bytes 16777216 | tf_op jit(solution)/shard_map/pallas_call | solution.py:813
  76.1 0.7 reshape.104
  76.8 0.6 pad.5.gates_hbm
  77.4 89.0 %shard_map.411 = (bf16[4,384,1024]{2,1,0:T(8,128)(2,1)}, bf16[4,384,1024]{2,1,0:T(8,128)(2,1)}, f32[4,8,384]{2,1,0:T(8,128)}, bf16[4,384,2048]{2,1,0:T(8,128)(2,...) custom-call(bf16[384,1024]{1,0:T(8,128)(2,1)} %get-tuple-element.44.rows_hbm.second_in, ...), custom_call_target="tpu_custom_call" | custom-call | flops 32212254720 | bytes 67108864 | tf_op jit(solution)/shard_map/pallas_call | solution.py:328
  166.5 0.0 reduce-scatter.3.cloned.1.call-update
  166.5 0.2 reduce-scatter.5.cloned.1.call-start
  166.7 76.4 %shard_map.412 = f32[4,128,1536]{2,1,0:T(8,128)} custom-call(bf16[1536,1024]{1,0:T(8,128)(2,1)} %bitcast.45, bf16[1536,1024]{1,0:T(8,128)(2,1)} %bitcast.44, bf16[1536,2048]{1,0:T(8,128)(2,1)} %bitcast.43, bf16[1536,4096]{1,0:T(8,128)(2,1)} %bitcast.42), custom_call_target="tpu_custom_call" | custom-call | flops 19327352832 | bytes 134217728 | tf_op jit(solution)/shard_map/pallas_call | solution.py:585
  243.1 0.0 copy-start.11
  243.1 0.0 copy-start.15
  243.2 0.0 copy-start.16
  243.2 0.0 copy-start.12
  243.2 0.0 copy-start.13
  243.2 0.0 copy-start.14
  243.2 0.0 reduce-scatter.3.cloned.1.call-done.back_rows
  243.2 0.0 reduce-scatter.5.cloned.1.call-update
  243.3 0.7 copy-done.11
  243.9 0.6 reshape.111.gate_grads
  244.6 0.0 copy-done.15
  244.6 0.1 copy.101
  244.7 0.8 constant_dynamic-slice_fusion
  245.4 0.1 copy.115
  245.5 0.0 copy-done.16
  245.5 0.1 copy.99
  245.6 0.1 copy.108
  245.7 0.0 copy-done.13
  245.7 0.7 copy.107
  246.4 0.0 copy-done.14
  246.4 0.7 copy.106
  247.1 68.3 %shard_map.413 = (f32[384,1024]{1,0:T(8,128)}, f32[6,32,512]{2,1,0:T(8,128)}, f32[1,32,128]{2,1,0:T(8,128)}) custom-call(bf16[384,1024]{1,0:T(8,128)(2,1)} %reduce-scatter.3.cloned.1.call-done.back_rows, f32[384,1024]{1,0:T(8,128)} %get-tuple-element.43.hidden, bf16[384,1024]{1,0:T(8,128)(2,1)} %cots.1, ...), custom_call_target="tpu_custom_call" | custom-call | flops 17179869184 | bytes 33554432 | tf_op jit(solution)/shard_map/pallas_call | solution.py:1240
  315.4 0.0 slice-start.1
  315.4 0.0 copy-start.5
  315.4 0.9 multiply_add_fusion.10
  316.4 0.6 copy.109
  317.0 0.6 copy.110
  317.6 0.6 copy.111
  318.3 0.9 slice_bitcast_fusion.1
  319.2 0.9 slice_bitcast_fusion
  320.1 1.4 multiply_add_fusion.8
  321.5 1.4 copy.112
  322.9 1.4 copy.113
  324.3 1.4 copy.114
  325.7 0.9 slice_bitcast_fusion.2
  326.6 0.0 copy-start.7
  326.6 0.0 copy-start.8
  326.6 0.0 copy-start.9
  326.7 1.8 multiply_add_fusion.6
  328.5 0.0 slice-done.1
  328.5 0.0 slice-start
  328.5 0.0 copy-start
  328.5 0.0 copy-start.1
  328.5 0.0 copy-start.2
  328.5 3.5 multiply_add_fusion.2
  332.0 0.9 multiply_add_fusion.4
  333.0 0.0 copy-done.1
  333.0 0.7 copy-done.2
  333.7 4.0 %multiply_add_fusion = (f32[4,128,1024]{2,1,0:T(8,128)}, f32[4,128,1024]{2,1,0:T(8,128)}, f32[4,128,1024]{2,1,0:T(8,128)}) fusion(f32[4,128,1024]{2,1,0:T(8,128)S(1)} %copy-done, f32[4,128,1024]{2,1,0:T(8,128)S(1)} %copy-done.1, f32[4,128,1024]{2,1,0:T(8,128)S(1)} %slice-done, f32[4,128,1024]{2,1,0:T(8,128)S(1)} %copy-done.2), kind=kLoop, calls=%fused_computation | loop fusion | flops 4718592 | bytes 14680064 | tf_op jit(solution)/shard_map/add | solution.py:50
  337.7 2.4 add_convert_fusion
  340.1 1.1 copy.125
  (31 shorter events, 0.1 us)
Async XLA Ops:
  7.2 236.0 %reduce-scatter.3.cloned.1.call-start = ((), (), s32[]{:S(2)}) async-start(), calls=%async_computation.2 | async-start | bytes 3932160 | tf_op jit(solution)/shard_map/reduce_scatter | solution.py:1351
  166.5 171.2 %reduce-scatter.5.cloned.1.call-start = ((), (), s32[]{:S(2)}) async-start(), calls=%async_computation.3 | async-start | bytes 3932160 | tf_op jit(solution)/shard_map/reduce_scatter | solution.py:1374
  243.1 0.8 copy-start.11
  243.1 1.4 copy-start.15
  243.2 2.3 copy-start.16
  243.2 2.4 copy-start.12
  243.2 2.5 copy-start.13
  243.2 3.2 copy-start.14
  247.0 79.6 %copy-start.10 = (f32[32,1024]{1,0:T(8,128)S(1)}, f32[32,1024]{1,0:T(8,128)}, u32[]{:S(2)}) copy-start(f32[32,1024]{1,0:T(8,128)} %param.41) | copy-start | bytes 393220
  247.0 81.4 %copy-start.6 = (f32[4,128,512]{2,1,0:T(8,128)S(1)}, f32[4,128,512]{2,1,0:T(8,128)}, u32[]{:S(2)}) copy-start(f32[4,128,512]{2,1,0:T(8,128)} %param.51) | copy-start | bytes 3145732
  315.4 13.1 %slice-start.1 = ((f32[4,128,1536]{2,1,0:T(8,128)}), f32[4,128,512]{2,1,0:T(8,128)S(1)}, s32[]{:S(2)}) async-start(f32[4,128,1536]{2,1,0:T(8,128)} %shard_map.412), calls=%async_computation.5 | async-start | bytes 2097152 | tf_op jit(solution)/shard_map/slice | solution.py:1365
  315.4 13.1 %copy-start.5 = (f32[4,128,512]{2,1,0:T(8,128)S(1)}, f32[4,128,512]{2,1,0:T(8,128)}, u32[]{:S(2)}) copy-start(f32[4,128,512]{2,1,0:T(8,128)} %param.53) | copy-start | bytes 3145732
  326.6 5.4 %copy-start.7 = (f32[32,2048]{1,0:T(8,128)S(1)}, f32[32,2048]{1,0:T(8,128)}, u32[]{:S(2)}) copy-start(f32[32,2048]{1,0:T(8,128)} %param.37) | copy-start | bytes 786436
  326.6 5.4 %copy-start.8 = (f32[32,2048]{1,0:T(8,128)S(1)}, f32[32,2048]{1,0:T(8,128)}, u32[]{:S(2)}) copy-start(f32[32,2048]{1,0:T(8,128)} %param.35) | copy-start | bytes 786436
  326.6 5.4 %copy-start.9 = (f32[32,2048]{1,0:T(8,128)S(1)}, f32[32,2048]{1,0:T(8,128)}, u32[]{:S(2)}) copy-start(f32[32,2048]{1,0:T(8,128)} %param.36) | copy-start | bytes 786436
  328.5 4.5 %slice-start = ((f32[4,128,1536]{2,1,0:T(8,128)}), f32[4,128,1024]{2,1,0:T(8,128)S(1)}, s32[]{:S(2)}) async-start(f32[4,128,1536]{2,1,0:T(8,128)} %shard_map.412), calls=%async_computation.4 | async-start | bytes 4194304 | tf_op jit(solution)/shard_map/slice | solution.py:1365
  328.5 4.5 %copy-start = (f32[4,128,1024]{2,1,0:T(8,128)S(1)}, f32[4,128,1024]{2,1,0:T(8,128)}, u32[]{:S(2)}) copy-start(f32[4,128,1024]{2,1,0:T(8,128)} %param.49) | copy-start | bytes 6291460
  328.5 4.5 %copy-start.1 = (f32[4,128,1024]{2,1,0:T(8,128)S(1)}, f32[4,128,1024]{2,1,0:T(8,128)}, u32[]{:S(2)}) copy-start(f32[4,128,1024]{2,1,0:T(8,128)} %param.47) | copy-start | bytes 6291460
  328.5 5.2 %copy-start.2 = (f32[4,128,1024]{2,1,0:T(8,128)S(1)}, f32[4,128,1024]{2,1,0:T(8,128)}, u32[]{:S(2)}) copy-start(f32[4,128,1024]{2,1,0:T(8,128)} %param.48) | copy-start | bytes 6291460
  333.7 4.0 %copy-start.3 = (f32[384,1024]{1,0:T(8,128)S(1)}, f32[384,1024]{1,0:T(8,128)}, u32[]{:S(2)}) copy-start(f32[384,1024]{1,0:T(8,128)} %get-tuple-element.43.hidden) | copy-start | bytes 4718596
  337.7 2.4 copy-start.4
Sparse Core Ops, SparseCore 0:
  166.6 59.0 reduce-scatter.2
  243.4 70.1 reduce-scatter.4
where the time goes:
time: 349 us; the launch traced here: 348 us
  Pallas kernels  298 us (85%)
  other arithmetic  18.7 us (5%)
  local copies, waits for them, and re-layouts  16.6 us (5%)
  between operations  14.3 us (4%)
    pallas_call x1, Pallas kernels, bank(): pl.pallas_call(functools.partial(bank_kernel, line), out_shape=(shape((li...  89 us
    pallas_call x1, Pallas kernels, bank_grads(): pl.pallas_call(bank_grads_kernel, out_shape=jax.ShapeDtypeStruct((experts...  76.4 us
    pallas_call x1, Pallas kernels, attend_back(): pl.pallas_call(functools.partial(attend_back_kernel, paired, line), out_s...  68.3 us
    pallas_call x1, Pallas kernels, attend(): pl.pallas_call(functools.partial(attend_kernel, line), out_shape=(shape((...  64.3 us
    unnamed x50, local copies, waits for them, and re-layouts  12.9 us
    add x6, other arithmetic, update(): DECAY * average + (1.0 - DECAY) * master_next  12.6 us
  transfers between devices with their start and end apart: 2, of which 0 were waited for; matrix products, arithmetic and copies ran while one was open for 7% of the time, Pallas kernels for 42%

commit v1 on v0

--- a/solution.py
+++ b/solution.py
@@ -53,7 +53,7 @@
 F32 = jnp.float32
 BF16 = jnp.bfloat16
 MESH = pl.DeviceIdType.MESH
-VMEM_MOST = 60 * 2**20
+VMEM_MOST = 61 * 2**20
 
 
 def contract(left, right, left_axis, right_axis):
@@ -64,6 +64,78 @@
 
 def visit_order(line):
     return [sorted(range(line), key=lambda s: (abs(s - z), s)) for z in range(line)]
+
+
+def line_gather(line, z, dp, source, landing, send_sem, recv_sem):
+    def copy(origin, block, sem, target):
+        return pltpu.make_async_remote_copy(
+            src_ref=origin,
+            dst_ref=landing.at[block],
+            send_sem=send_sem.at[sem],
+            recv_sem=recv_sem.at[block],
+            device_id=(dp, target),
+            device_id_type=MESH,
+        )
+
+    def start():
+        @pl.when(z < line - 1)
+        def _():
+            copy(source, z, line, z + 1).start()
+
+        @pl.when(z > 0)
+        def _():
+            copy(source, z, line + 1, z - 1).start()
+
+    def pass_on(apart):
+        low = jnp.maximum(z - apart, 0)
+        high = jnp.minimum(z + apart, line - 1)
+
+        @pl.when(z - apart >= 0)
+        def _():
+            copy(source, low, low, z).wait_recv()
+
+            @pl.when(z < line - 1)
+            def _():
+                copy(landing.at[low], low, low, z + 1).start()
+
+        @pl.when(z + apart < line)
+        def _():
+            copy(source, high, high, z).wait_recv()
+
+            @pl.when(z > 0)
+            def _():
+                copy(landing.at[high], high, high, z - 1).start()
+
+    def finish():
+        @pl.when(z < line - 1)
+        def _():
+            copy(source, z, line, z + 1).wait_send()
+
+        @pl.when(z > 0)
+        def _():
+            copy(source, z, line + 1, z - 1).wait_send()
+
+        for s in range(line):
+
+            @pl.when(((s < z) & (z < line - 1)) | ((s > z) & (z > 0)))
+            def _(s=s):
+                copy(source, s, s, z).wait_send()
+
+    return start, pass_on, finish
+
+
+def pass_steps(line, experts):
+    steps = []
+    for z in range(line):
+        order = visit_order(line)[z]
+        for apart in range(1, line):
+            met = [k for k in range(line) if abs(order[k] - z) == apart]
+            if not met:
+                continue
+            forwards = (z - apart >= 0 and z < line - 1) or (z + apart < line and z > 0)
+            early = experts // 2 if forwards and apart > 1 else 0
+            steps.append((z, met[0] * experts - early, apart))
+    return steps
 
 
 def pick(table, row, column):
@@ -72,300 +144,6 @@
         for c in range(len(table[0])):
             value = jnp.where((row == r) & (column == c), jnp.int32(table[r][c]), value)
     return value
-
-
-def bank_kernel(
-    line,
-    rows_hbm,
-    cots_hbm,
-    gates_hbm,
-    up_hbm,
-    down_hbm,
-    mix_hbm,
-    back_hbm,
-    gate_grads_hbm,
-    gated_hbm,
-    inner_hbm,
-    rows_all_hbm,
-    rows,
-    cots,
-    gates,
-    gate_grads,
-    gate_grads_sent,
-    up,
-    down,
-    mix_sum,
-    back_sum,
-    stage,
-    gated,
-    inner,
-    columns,
-    row_send,
-    row_recv,
-    gate_send,
-    gate_recv,
-    weight_sem,
-    local_sem,
-    out_sem,
-    grad_send,
-    grad_recv,
-):
-    dp = lax.axis_index("dp")
-    z = lax.axis_index("expert")
-    experts, width, ff_width = down.shape
-
-    def weight_copies(e):
-        return (
-            pltpu.make_async_copy(up_hbm.at[e], up.at[e], weight_sem.at[0, e]),
-            pltpu.make_async_copy(down_hbm.at[e], down.at[e], weight_sem.at[1, e]),
-        )
-
-    for e in range(experts):
-        for copy in weight_copies(e):
-            copy.start()
-    own_rows = pltpu.make_async_copy(rows_hbm, rows.at[z], local_sem.at[0])
-    own_rows.start()
-    all_cots = pltpu.make_async_copy(cots_hbm, cots, local_sem.at[1])
-    all_cots.start()
-    own_gates = pltpu.make_async_copy(gates_hbm.at[z], gates.at[z], local_sem.at[2])
-    own_gates.start()
-
-    barrier = pltpu.get_barrier_semaphore()
-    for step in range(1, line):
-        pl.semaphore_signal(
-            barrier, inc=1, device_id=(dp, lax.rem(z + step, line)), device_id_type=MESH
-        )
-    pl.semaphore_wait(barrier, line - 1)
-
-    def row_copy(source, block, sem, target):
-        return pltpu.make_async_remote_copy(
-            src_ref=source,
-            dst_ref=rows.at[block],
-            send_sem=row_send.at[sem],
-            recv_sem=row_recv.at[block],
-            device_id=(dp, target),
-            device_id_type=MESH,
-        )
-
-    @pl.when(z < line - 1)
-    def _():
-        row_copy(rows_hbm, z, line, z + 1).start()
-
-    @pl.when(z > 0)
-    def _():
-        row_copy(rows_hbm, z, line + 1, z - 1).start()
-
-    def gate_copy(step):
-        peer = lax.rem(z + step, line)
-        return pltpu.make_async_remote_copy(
-            src_ref=gates_hbm.at[peer],
-            dst_ref=gates.at[z],
-            send_sem=gate_send.at[step],
-            recv_sem=gate_recv.at[step],
-            device_id=(dp, peer),
-            device_id_type=MESH,
-        )
-
-    for step in range(1, line):
-        gate_copy(step).start()
-    own_rows.wait()
-    all_cots.wait()
-    own_gates.wait()
-    for step in range(1, line):
-        gate_copy(step).wait()
-
-    order = visit_order(line)
-
-    def out_copies(slot, block):
-        return (
-            pltpu.make_async_copy(stage.at[slot, 0], mix_hbm.at[block], out_sem.at[slot, 0]),
-            pltpu.make_async_copy(stage.at[slot, 1], back_hbm.at[block], out_sem.at[slot, 1]),
-            pltpu.make_async_copy(gated.at[slot], gated_hbm.at[block], out_sem.at[slot, 2]),
-            pltpu.make_async_copy(inner.at[slot], inner_hbm.at[block], out_sem.at[slot, 3]),
-        )
-
-    def grad_copy(block, step):
-        return pltpu.make_async_remote_copy(
-            src_ref=gate_grads_sent.at[block],
-            dst_ref=gate_grads.at[z],
-            send_sem=grad_send.at[block],
-            recv_sem=grad_recv.at[z],
-            device_id=(dp, block),
-            device_id_type=MESH,
-        )
-
-    def visit(k, _):
-        block = pick(order, z, k)
-        slot = lax.rem(k, 2)
-        apart = jnp.abs(block - z)
-        previous = pick(order, z, jnp.maximum(k - 1, 0))
-        first = (k > 0) & (apart != jnp.abs(previous - z))
-        below = z - apart
-        above = z + apart
-
-        @pl.when(first & (below >= 0))
-        def _():
-            low = jnp.maximum(below, 0)
-            row_copy(rows_hbm, low, low, z).wait_recv()
-
-            @pl.when(z < line - 1)
-            def _():
-                row_copy(rows.at[low], low, low, z + 1).start()
-
-        @pl.when(first & (above < line))
-        def _():
-            high = jnp.minimum(above, line - 1)
-            row_copy(rows_hbm, high, high, z).wait_recv()
-
-            @pl.when(z > 0)
-            def _():
-                row_copy(rows.at[high], high, high, z - 1).start()
-
-        @pl.when(k >= 2)
-        def _():
-            for copy in out_copies(slot, pick(order, z, jnp.maximum(k - 2, 0))):
-                copy.wait()
-
-        mix_sum[...] = jnp.zeros_like(mix_sum)
-        back_sum[...] = jnp.zeros_like(back_sum)
-        columns[...] = jnp.zeros_like(columns)
-        gate_columns = gates[block].T
-        lane = lax.broadcasted_iota(jnp.int32, gate_columns.shape, 1)
-        wide_lane = lax.broadcasted_iota(jnp.int32, columns.shape, 1)
-
-        def expert(e, _):
-            @pl.when(k == 0)
-            def _():
-                for copy in weight_copies(e):
-                    copy.wait()
-
-            gate_col = jnp.sum(jnp.where(lane == e, gate_columns, 0.0), axis=1, keepdims=True)
-            both = contract(rows[block], up[e], 1, 0)
-            returned = contract(cots[block], down[e], 1, 0)
-            gate_part = both[:, :ff_width]
-            up_part = both[:, ff_width:]
-            sigmoid_gate = jax.nn.sigmoid(gate_part)
-            silu_gate = gate_part * sigmoid_gate
-            active = silu_gate * up_part
-            gated_part = (active * gate_col).astype(BF16)
-            gated[slot, :, pl.ds(pl.multiple_of(e * ff_width, ff_width), ff_width)] = gated_part
-            mix_sum[...] += contract(gated_part, down[e], 1, 1)
-            gate_grad = jnp.sum(active * returned, axis=1, keepdims=True)
-            columns[...] = jnp.where(wide_lane == e, gate_grad, columns[...])
-            scaled = returned * gate_col
-            grad_gate = scaled * up_part * (sigmoid_gate * (1.0 + gate_part * (1.0 - sigmoid_gate)))
-            grad_up = scaled * silu_gate
-            grads = jnp.concatenate([grad_gate, grad_up], axis=1).astype(BF16)
-            inner[slot, :, pl.ds(pl.multiple_of(e * 2 * ff_width, ff_width), 2 * ff_width)] = grads
-            back_sum[...] += contract(grads, up[e], 1, 1)
-            return 0
-
-        lax.fori_loop(0, experts, expert, 0)
-        stage[slot, 0] = mix_sum[...].astype(BF16)
-        stage[slot, 1] = back_sum[...].astype(BF16)
-        for copy in out_copies(slot, block):
-            copy.start()
-        gate_grads_sent[block] = columns[...].T[: gate_grads.shape[1]]
-
-        @pl.when(block == z)
-        def _():
-            gate_grads[z] = gate_grads_sent[z]
-
-        @pl.when(block != z)
-        def _():
-            grad_copy(block, 0).start()
-
-        return 0
-
-    lax.fori_loop(0, line, visit, 0)
-    for k in (line - 2, line - 1):
-        for copy in out_copies(k % 2, pick(order, z, k)):
-            copy.wait()
-
-    @pl.when(z < line - 1)
-    def _():
-        row_copy(rows_hbm, z, line, z + 1).wait_send()
-
-    @pl.when(z > 0)
-    def _():
-        row_copy(rows_hbm, z, line + 1, z - 1).wait_send()
-
-    for s in range(line):
-
-        @pl.when(((s < z) & (z < line - 1)) | ((s > z) & (z > 0)))
-        def _(s=s):
-            row_copy(rows_hbm, s, s, z).wait_send()
-
-        @pl.when(s != z)
-        def _(s=s):
-            grad_copy(s, 0).wait_send()
-            pltpu.make_async_remote_copy(
-                src_ref=gate_grads_sent.at[s],
-                dst_ref=gate_grads.at[s],
-                send_sem=grad_send.at[s],
-                recv_sem=grad_recv.at[s],
-                device_id=(dp, z),
-                device_id_type=MESH,
-            ).wait_recv()
-
-    last = (
-        pltpu.make_async_copy(rows, rows_all_hbm, local_sem.at[0]),
-        pltpu.make_async_copy(gate_grads, gate_grads_hbm, local_sem.at[1]),
-    )
-    for copy in last:
-        copy.start()
-    for copy in last:
-        copy.wait()
-
-
-def bank(rows, cots, gates, up, down, line):
-    tokens, width = rows.shape
-    experts, _, ff_width = down.shape
-    shape = jax.ShapeDtypeStruct
-    held = gates.shape[1:]
-    anywhere = pl.BlockSpec(memory_space=pl.ANY)
-    work = 10 * line * tokens * experts * width * ff_width
-    return pl.pallas_call(
-        functools.partial(bank_kernel, line),
-        out_shape=(
-            shape((line, tokens, width), BF16),
-            shape((line, tokens, width), BF16),
-            shape((line,) + held, F32),
-            shape((line, tokens, experts * ff_width), BF16),
-            shape((line, tokens, experts * 2 * ff_width), BF16),
-            shape((line, tokens, width), BF16),
-        ),
-        in_specs=[anywhere] * 5,
-        out_specs=(anywhere,) * 6,
-        scratch_shapes=[
-            pltpu.VMEM((line, tokens, width), BF16),
-            pltpu.VMEM((line, tokens, width), BF16),
-            pltpu.VMEM((line,) + held, F32),
-            pltpu.VMEM((line,) + held, F32),
-            pltpu.VMEM((line,) + held, F32),
-            pltpu.VMEM(up.shape, BF16),
-            pltpu.VMEM(down.shape, BF16),
-            pltpu.VMEM((tokens, width), F32),
-            pltpu.VMEM((tokens, width), F32),
-            pltpu.VMEM((2, 2, tokens, width), BF16),
-            pltpu.VMEM((2, tokens, experts * ff_width), BF16),
-            pltpu.VMEM((2, tokens, experts * 2 * ff_width), BF16),
-            pltpu.VMEM((tokens, 128), F32),
-            pltpu.SemaphoreType.DMA((line + 2,)),
-            pltpu.SemaphoreType.DMA((line,)),
-            pltpu.SemaphoreType.DMA((line,)),
-            pltpu.SemaphoreType.DMA((line,)),
-            pltpu.SemaphoreType.DMA((2, experts)),
-            pltpu.SemaphoreType.DMA((3,)),
-            pltpu.SemaphoreType.DMA((2, 4)),
-            pltpu.SemaphoreType.DMA((line,)),
-            pltpu.SemaphoreType.DMA((line,)),
-        ],
-        compiler_params=pltpu.CompilerParams(
-            collective_id=1, has_side_effects=True, vmem_limit_bytes=VMEM_MOST
-        ),
-        cost_estimate=pl.CostEstimate(flops=work, bytes_accessed=2**26, transcendentals=0),
-    )(rows, cots, gates, up, down)
 
 
 def weight_grads_kernel(rows, cots, gated, inner, up_grad, down_grad):
@@ -421,8 +199,6 @@
     grads,
     core_sum,
     first_sum,
-    last_sum,
-    total,
     load_sem,
     send_sem,
     recv_sem,
@@ -481,11 +257,6 @@
             return send(1, e, core_sum.at[e, :, 1 - x], first_sum.at[e], x_peer)
         return send(1, e, core_sum.at[e, 1 - y], first_sum.at[e], y_peer)
 
-    def last_send(e, along_x):
-        if along_x:
-            return send(2, e, first_sum.at[e, 1 - x], last_sum.at[e], x_peer)
-        return send(2, e, first_sum.at[e, 1 - y], last_sum.at[e], y_peer)
-
     def by_parity(e, act):
         even = lax.rem(e, 2) == 0
 
@@ -514,18 +285,9 @@
                 first_sum[e, other] = (
                     kept.astype(F32) + first_sum[e, other].astype(F32)
                 ).astype(BF16)
-            last_send(e, not even).start()
 
         by_parity(e, act)
-
-    def after_last(e):
-        def act(even):
-            last_send(e, not even).wait_recv()
-            kept = first_sum[e, y] if even else first_sum[e, x]
-            total[e] = kept.astype(F32) + last_sum[e].astype(F32)
-
-        by_parity(e, act)
-        pltpu.make_async_copy(total.at[e], sum_hbm.at[e], out_sem.at[e]).start()
+        pltpu.make_async_copy(first_sum.at[e], sum_hbm.at[e], out_sem.at[e]).start()
 
     def step(e, _):
         slot = lax.rem(e, 2)
@@ -565,15 +327,10 @@
 
     for e in range(max(experts - 3, 0), experts):
         after_first(e)
-        if e - 2 >= 0:
-            after_last(e - 2)
-    for e in range(max(experts - 2, 0), experts):
-        after_last(e)
     for e in range(experts):
         core_send(e).wait_send()
         first_send(e, e % 2 == 0).wait_send()
-        last_send(e, e % 2 == 1).wait_send()
-        pltpu.make_async_copy(total.at[e], sum_hbm.at[e], out_sem.at[e]).wait()
+        pltpu.make_async_copy(first_sum.at[e], sum_hbm.at[e], out_sem.at[e]).wait()
 
 
 def bank_grads(rows, cots, gated, inner, experts):
@@ -584,7 +341,7 @@
     anywhere = pl.BlockSpec(memory_space=pl.ANY)
     return pl.pallas_call(
         bank_grads_kernel,
-        out_shape=jax.ShapeDtypeStruct((experts, block_rows, lanes), F32),
+        out_shape=jax.ShapeDtypeStruct((experts, 2, block_rows, lanes), BF16),
         in_specs=[anywhere] * 4,
         out_specs=anywhere,
         scratch_shapes=[
@@ -595,11 +352,9 @@
             pltpu.VMEM((experts, 2, 2, 2, block_rows, lanes), BF16),
             pltpu.VMEM((experts, 2, 2, block_rows, lanes), BF16),
             pltpu.VMEM((experts, 2, block_rows, lanes), BF16),
-            pltpu.VMEM((experts, block_rows, lanes), BF16),
-            pltpu.VMEM((experts, block_rows, lanes), F32),
             pltpu.SemaphoreType.DMA((2, 3)),
-            pltpu.SemaphoreType.DMA((3, experts)),
-            pltpu.SemaphoreType.DMA((3, experts)),
+            pltpu.SemaphoreType.DMA((2, experts)),
+            pltpu.SemaphoreType.DMA((2, experts)),
             pltpu.SemaphoreType.DMA((experts,)),
         ],
         compiler_params=pltpu.CompilerParams(
@@ -617,64 +372,6 @@
 UNIT = 512
 
 
-def line_gather(line, z, dp, source, landing, send_sem, recv_sem):
-    def copy(origin, block, sem, target):
-        return pltpu.make_async_remote_copy(
-            src_ref=origin,
-            dst_ref=landing.at[block],
-            send_sem=send_sem.at[sem],
-            recv_sem=recv_sem.at[block],
-            device_id=(dp, target),
-            device_id_type=MESH,
-        )
-
-    def start():
-        @pl.when(z < line - 1)
-        def _():
-            copy(source, z, line, z + 1).start()
-
-        @pl.when(z > 0)
-        def _():
-            copy(source, z, line + 1, z - 1).start()
-
-    def pass_on(apart):
-        low = jnp.maximum(z - apart, 0)
-        high = jnp.minimum(z + apart, line - 1)
-
-        @pl.when(z - apart >= 0)
-        def _():
-            copy(source, low, low, z).wait_recv()
-
-            @pl.when(z < line - 1)
-            def _():
-                copy(landing.at[low], low, low, z + 1).start()
-
-        @pl.when(z + apart < line)
-        def _():
-            copy(source, high, high, z).wait_recv()
-
-            @pl.when(z > 0)
-            def _():
-                copy(landing.at[high], high, high, z - 1).start()
-
-    def finish():
-        @pl.when(z < line - 1)
-        def _():
-            copy(source, z, line, z + 1).wait_send()
-
-        @pl.when(z > 0)
-        def _():
-            copy(source, z, line + 1, z - 1).wait_send()
-
-        for s in range(line):
-
-            @pl.when(((s < z) & (z < line - 1)) | ((s > z) & (z > 0)))
-            def _(s=s):
-                copy(source, s, s, z).wait_send()
-
-    return start, pass_on, finish
-
-
 def swap_halves(value):
     lane = lax.broadcasted_iota(jnp.int32, value.shape, 1)
     half = HEAD_DIM // 2
@@ -702,8 +399,10 @@
     return pl.ds(pl.multiple_of(start, 128), size)
 
 
-def attend_kernel(
+def front_kernel(
     line,
+    prompt,
+    late,
     tokens,
     cots_hbm,
     gain_rows,
@@ -714,6 +413,8 @@
     cosine,
     sine,
     bias,
+    up_hbm,
+    down_hbm,
     first_in,
     queries,
     keys,
@@ -724,22 +425,77 @@
     gate_rows,
     log_totals,
     cots_all,
-    send_sem,
-    recv_sem,
-    own_sem,
+    mix_all,
+    mix_late,
+    back_hbm,
+    gate_grads_hbm,
+    gated_hbm,
+    inner_hbm,
+    rows_all_hbm,
+    cots,
+    rows,
+    gates_own,
+    gates,
+    gate_grads,
+    gate_grads_sent,
+    up,
+    down,
+    projected,
+    stage,
+    mix_stage,
+    gated,
+    inner,
+    columns,
+    cot_send,
+    cot_recv,
+    row_send,
+    row_recv,
+    gate_send,
+    gate_recv,
+    weight_sem,
+    local_sem,
+    out_sem,
+    grad_send,
+    grad_recv,
+    mix_send,
+    mix_recv,
 ):
     dp = lax.axis_index("dp")
     z = lax.axis_index("expert")
-    start, pass_on, finish = line_gather(line, z, dp, cots_hbm, cots_all, send_sem, recv_sem)
+    experts, _, ff_width = down_hbm.shape
+    start_cots, pass_cots, finish_cots = line_gather(
+        line, z, dp, cots_hbm, cots_all, cot_send, cot_recv
+    )
+    start_rows, pass_rows, finish_rows = line_gather(
+        line, z, dp, second_in, rows, row_send, row_recv
+    )
+
+    def weight_copies(e):
+        return (
+            pltpu.make_async_copy(
+                up_hbm.at[e],
+                up.at[:, pl.ds(pl.multiple_of(e * 2 * ff_width, ff_width), 2 * ff_width)],
+                weight_sem.at[0, e],
+            ),
+            pltpu.make_async_copy(
+                down_hbm.at[e],
+                down.at[:, pl.ds(pl.multiple_of(e * ff_width, ff_width), ff_width)],
+                weight_sem.at[1, e],
+            ),
+        )
+
     barrier = pltpu.get_barrier_semaphore()
     for step in range(1, line):
         pl.semaphore_signal(
             barrier, inc=1, device_id=(dp, lax.rem(z + step, line)), device_id_type=MESH
         )
     pl.semaphore_wait(barrier, line - 1)
-    start()
-    own = pltpu.make_async_copy(cots_hbm, cots_all.at[z], own_sem)
-    own.start()
+    start_cots()
+    cots_in = pltpu.make_async_copy(cots_hbm, cots, local_sem.at[2])
+    cots_in.start()
+    for e in range(experts):
+        for copy in weight_copies(e):
+            copy.start()
 
     query_end = HEADS * HEAD_DIM
     key_end = query_end + KV_HEADS * HEAD_DIM
@@ -747,48 +503,74 @@
     factor = lax.rsqrt(jnp.mean(token_rows * token_rows, axis=1, keepdims=True) + EPS)
     first_in[...] = (token_rows * factor * gain_rows[0:1]).astype(BF16)
     log_totals[...] = jnp.zeros_like(log_totals)
+    cots_in.wait()
+    own_cots = pltpu.make_async_copy(cots, cots_all.at[z], local_sem.at[0])
+    own_cots.start()
+
+    def project(i, _):
+        at = lanes_at(i * UNIT, UNIT)
+        projected[:, at] = contract(first_in[...], heads_in[:, at], 1, 0)
+        return 0
+
+    lax.fori_loop(0, heads_in.shape[1] // UNIT, project, 0)
 
     def pair(j, _):
         for side in range(2):
-            wide = contract(
-                first_in[...], heads_in[:, lanes_at((2 * j + side) * PAIR, PAIR)], 1, 0
-            )
-            queries[:, lanes_at((2 * j + side) * PAIR, PAIR)] = (
-                wide * cosine[...] + swap_halves(wide) * sine[...]
-            ).astype(BF16)
-        wide = contract(first_in[...], heads_in[:, lanes_at(query_end + j * PAIR, PAIR)], 1, 0)
+            at = lanes_at((2 * j + side) * PAIR, PAIR)
+            wide = projected[:, at]
+            queries[:, at] = (wide * cosine[...] + swap_halves(wide) * sine[...]).astype(BF16)
+        wide = projected[:, lanes_at(query_end + j * PAIR, PAIR)]
         keys[:, lanes_at(j * PAIR, PAIR)] = (
             wide * cosine[...] + swap_halves(wide) * sine[...]
         ).astype(BF16)
-        values[:, lanes_at(j * PAIR, PAIR)] = contract(
-            first_in[...], heads_in[:, lanes_at(key_end + j * PAIR, PAIR)], 1, 0
-        ).astype(BF16)
+        values[:, lanes_at(j * PAIR, PAIR)] = projected[
+            :, lanes_at(key_end + j * PAIR, PAIR)
+        ].astype(BF16)
+        heads = [(side, member) for side in range(2) for member in range(2)]
+        groups = [queries[:, lanes_at((2 * j + side) * PAIR, PAIR)] for side in range(2)]
+        key_sides = [sides(keys[:, lanes_at(j * PAIR, PAIR)], side, SCALE) for side in range(2)]
+        value_sides = [sides(values[:, lanes_at(j * PAIR, PAIR)], side, None) for side in range(2)]
+        parts = ((0, prompt, prompt), (prompt, groups[0].shape[0], groups[0].shape[0]))
+
+        def scores_of(side, member):
+            return [
+                contract(groups[side][begin:end], key_sides[side][member][:seen], 1, 1)
+                + bias[begin:end, :seen]
+                for begin, end, seen in parts
+            ]
+
+        lane = lax.broadcasted_iota(jnp.int32, log_totals.shape, 1)
+        added = jnp.zeros(log_totals.shape, F32)
+        sums = [0.0, 0.0]
+        scores = scores_of(*heads[0])
+        for number, (side, member) in enumerate(heads):
+            following = scores_of(*heads[number + 1]) if number + 1 < len(heads) else None
+            mixed = []
+            totals = []
+            for part, (_, _, seen) in zip(scores, parts):
+                peak = jnp.max(part, axis=1, keepdims=True)
+                powers = jnp.exp(part - peak)
+                amount = jnp.sum(powers, axis=1, keepdims=True)
+                weights = (powers * (1.0 / amount)).astype(BF16)
+                totals.append(peak + jnp.log(amount))
+                mixed.append(contract(weights, value_sides[side][member][:seen], 1, 0))
+            sums[side] = sums[side] + jnp.concatenate(mixed, axis=0)
+            added = jnp.where(lane == 4 * j + number, jnp.concatenate(totals, axis=0), added)
+            scores = following
+        log_totals[...] += added
         for side in range(2):
-            group = queries[:, lanes_at((2 * j + side) * PAIR, PAIR)]
-            key_sides = sides(keys[:, lanes_at(j * PAIR, PAIR)], side, SCALE)
-            value_sides = sides(values[:, lanes_at(j * PAIR, PAIR)], side, None)
-            total = jnp.zeros(group.shape, F32)
-            for member in range(2):
-                scores = contract(group, key_sides[member], 1, 1) + bias[...]
-                peak = jnp.max(scores, axis=1, keepdims=True)
-                powers = jnp.exp(scores - peak)
-                amount = jnp.sum(powers, axis=1, keepdims=True)
-                lane = lax.broadcasted_iota(jnp.int32, log_totals.shape, 1)
-                log_totals[...] = jnp.where(
-                    lane == 4 * j + 2 * side + member, peak + jnp.log(amount), log_totals[...]
-                )
-                weights = (powers * (1.0 / amount)).astype(BF16)
-                total = total + contract(weights, value_sides[member], 1, 0)
-            attended[:, lanes_at((2 * j + side) * PAIR, PAIR)] = total.astype(BF16)
+            attended[:, lanes_at((2 * j + side) * PAIR, PAIR)] = sums[side].astype(BF16)
         return 0
 
     lax.fori_loop(0, KV_HEADS // 2, pair, 0)
-    pass_on(1)
     hidden_rows = token_rows + contract(attended[...], heads_out[...], 1, 1)
     hidden[...] = hidden_rows
     factor = lax.rsqrt(jnp.mean(hidden_rows * hidden_rows, axis=1, keepdims=True) + EPS)
     second = (hidden_rows * factor * gain_rows[1:2]).astype(BF16)
     second_in[...] = second
+    start_rows()
+    own_rows = pltpu.make_async_copy(second_in, rows.at[z], local_sem.at[1])
+    own_rows.start()
     logits = contract(router_rows[...], second, 1, 1)
     expert = lax.broadcasted_iota(jnp.int32, logits.shape, 0)
     named = expert == route_rows[0:1]
@@ -796,22 +578,283 @@
         named = named | (expert == route_rows[k : k + 1])
     peak = jnp.max(jnp.where(named, logits, -1e30), axis=0, keepdims=True)
     powers = jnp.where(named, jnp.exp(jnp.where(named, logits, peak) - peak), 0.0)
-    gate_rows[...] = powers / jnp.sum(powers, axis=0, keepdims=True)
-    for apart in range(2, line):
-        pass_on(apart)
-    finish()
-    own.wait()
-
-
-def attend(tokens, cots, gain_rows, heads_in, heads_out, router_rows, route_rows, tables, line):
+    gate_values = powers / jnp.sum(powers, axis=0, keepdims=True)
+    gate_rows[...] = gate_values
+    gates_own[...] = jnp.zeros_like(gates_own)
+    for peer in range(line):
+        gates_own[peer, :experts] = gate_values[peer * experts : (peer + 1) * experts]
+    gates[z] = gates_own[z]
+    def gate_copy(step):
+        peer = lax.rem(z + step, line)
+        return pltpu.make_async_remote_copy(
+            src_ref=gates_own.at[peer],
+            dst_ref=gates.at[z],
+            send_sem=gate_send.at[step],
+            recv_sem=gate_recv.at[step],
+            device_id=(dp, peer),
+            device_id_type=MESH,
+        )
+
+    for step in range(1, line):
+        gate_copy(step).start()
+    own_rows.wait()
+    own_cots.wait()
+    pass_cots(1)
+    for step in range(1, line):
+        gate_copy(step).wait()
+
+    order = visit_order(line)
+
+    def out_copies(slot, block):
+        return (
+            pltpu.make_async_copy(stage.at[slot], back_hbm.at[block], out_sem.at[slot, 0]),
+            pltpu.make_async_copy(gated.at[slot], gated_hbm.at[block], out_sem.at[slot, 1]),
+            pltpu.make_async_copy(inner.at[slot], inner_hbm.at[block], out_sem.at[slot, 2]),
+        )
+
+    def mix_copy(block, source, target):
+        return pltpu.make_async_remote_copy(
+            src_ref=mix_stage.at[block],
+            dst_ref=mix_all.at[source],
+            send_sem=mix_send.at[block],
+            recv_sem=mix_recv.at[source],
+            device_id=(dp, target),
+            device_id_type=MESH,
+        )
+
+    def own_mix():
+        return pltpu.make_async_copy(mix_stage.at[z], mix_all.at[z], local_sem.at[3])
+
+    def late_mix(side):
+        return pltpu.make_async_copy(
+            mix_stage.at[side * (line - 1)], mix_late.at[side], local_sem.at[4 + side]
+        )
+
+    def at_end(block):
+        return (block == 0) | (block == line - 1)
+
+    def grad_copy(block, step):
+        return pltpu.make_async_remote_copy(
+            src_ref=gate_grads_sent.at[block],
+            dst_ref=gate_grads.at[z],
+            send_sem=grad_send.at[block],
+            recv_sem=grad_recv.at[z],
+            device_id=(dp, block),
+            device_id_type=MESH,
+        )
+
+    def visit(k, _):
+        block = pick(order, z, k)
+        slot = lax.rem(k, 2)
+        @pl.when(k >= 2)
+        def _():
+            for copy in out_copies(slot, pick(order, z, jnp.maximum(k - 2, 0))):
+                copy.wait()
+
+        cot_load = pltpu.make_async_copy(cots_all.at[block], cots, local_sem.at[2])
+        gate_columns = gates[block].T
+        tile = min(ff_width, 256)
+        def arrive(e):
+            step = k * experts + e
+            apart = jnp.int32(0)
+            for at_z, at_step, distance in pass_steps(line, experts):
+                apart = jnp.where((z == at_z) & (step == at_step), distance, apart)
+
+            @pl.when(apart > 0)
+            def _():
+                pass_rows(apart)
+
+            if line > 2:
+
+                @pl.when(apart == 1)
+                def _():
+                    pass_cots(2)
+
+            @pl.when(apart > 2)
+            def _():
+                pass_cots(apart)
+
+            @pl.when((k > 0) & (e == 0))
+            def _():
+                cot_load.start()
+                cot_load.wait()
+
+        def products(e, at):
+            gate_at = pl.multiple_of(2 * e * ff_width + at, tile)
+            up_at = pl.multiple_of((2 * e + 1) * ff_width + at, tile)
+            down_at = pl.multiple_of(e * ff_width + at, tile)
+            return (
+                contract(rows[block], up[:, pl.ds(gate_at, tile)], 1, 0),
+                contract(rows[block], up[:, pl.ds(up_at, tile)], 1, 0),
+                contract(cots[...], down[:, pl.ds(down_at, tile)], 1, 0),
+            )
+
+        narrow_lane = lax.broadcasted_iota(jnp.int32, gate_columns.shape, 1)
+        wide_lane = lax.broadcasted_iota(jnp.int32, columns.shape, 1)
+        several = experts // 2
+        columns[...] = jnp.zeros_like(columns)
+
+        def half(part, _):
+            begin = part * several
+            arrive(begin)
+
+            @pl.when(k == 0)
+            def _():
+                for e in range(several):
+                    for copy in weight_copies(begin + e):
+                        copy.wait()
+
+            tiles = [(e, at) for e in range(several) for at in range(0, ff_width, tile)]
+            ready = products(begin + tiles[0][0], tiles[0][1])
+            sums = [0.0] * several
+            for number, (near, at) in enumerate(tiles):
+                following = None
+                if number + 1 < len(tiles):
+                    following = products(begin + tiles[number + 1][0], tiles[number + 1][1])
+                e = begin + near
+                gate_part, up_part, returned = ready
+                gate_col = jnp.sum(
+                    jnp.where(narrow_lane == e, gate_columns, 0.0), axis=1, keepdims=True
+                )
+                sigmoid_gate = jax.nn.sigmoid(gate_part)
+                silu_gate = gate_part * sigmoid_gate
+                active = silu_gate * up_part
+                sums[near] = sums[near] + jnp.sum(active * returned, axis=1, keepdims=True)
+                scaled = returned * gate_col
+                grad_gate = scaled * up_part * (sigmoid_gate + silu_gate * (1.0 - sigmoid_gate))
+                gate_at = pl.multiple_of(2 * e * ff_width + at, tile)
+                up_at = pl.multiple_of((2 * e + 1) * ff_width + at, tile)
+                down_at = pl.multiple_of(e * ff_width + at, tile)
+                gated[slot, :, pl.ds(down_at, tile)] = (active * gate_col).astype(BF16)
+                inner[slot, :, pl.ds(gate_at, tile)] = grad_gate.astype(BF16)
+                inner[slot, :, pl.ds(up_at, tile)] = (scaled * silu_gate).astype(BF16)
+                ready = following
+            value = columns[...]
+            for near in range(several):
+                value = jnp.where(wide_lane == begin + near, sums[near], value)
+            columns[...] = value
+            return 0
+
+        lax.fori_loop(0, 2, half, 0)
+        mix_stage[block] = contract(gated[slot], down[...], 1, 1).astype(BF16)
+
+        @pl.when(block == z)
+        def _():
+            own_mix().start()
+
+        if late:
+            for side in range(2):
+
+                @pl.when((block != z) & (block == side * (line - 1)))
+                def _(side=side):
+                    late_mix(side).start()
+
+            @pl.when((block != z) & jnp.logical_not(at_end(block)))
+            def _():
+                mix_copy(block, z, block).start()
+
+        else:
+
+            @pl.when(block != z)
+            def _():
+                mix_copy(block, z, block).start()
+
+        stage[slot] = contract(inner[slot], up[...], 1, 1).astype(BF16)
+        for copy in out_copies(slot, block):
+            copy.start()
+        gate_grads_sent[block] = columns[...].T[: gate_grads.shape[1]]
+
+        @pl.when(block == z)
+        def _():
+            gate_grads[z] = gate_grads_sent[z]
+
+        @pl.when(block != z)
+        def _():
+            grad_copy(block, 0).start()
+
+        return 0
+
+    lax.fori_loop(0, line, visit, 0)
+    for k in range(max(line - 2, 0), line):
+        for copy in out_copies(k % 2, pick(order, z, k)):
+            copy.wait()
+
+    finish_rows()
+    finish_cots()
+    own_mix().wait()
+    if late:
+        for side in range(2):
+
+            @pl.when(z != side * (line - 1))
+            def _(side=side):
+                late_mix(side).wait()
+
+    for s in range(line):
+        send_ends = late and s in (0, line - 1)
+
+        @pl.when(z != s)
+        def _(s=s, send_ends=send_ends):
+            if not send_ends:
+                mix_copy(s, s, z).wait_send()
+            if late:
+
+                @pl.when(jnp.logical_not(at_end(z)))
+                def _():
+                    mix_copy(s, s, z).wait_recv()
+
+            else:
+                mix_copy(s, s, z).wait_recv()
+
+    for s in range(line):
+
+        @pl.when(s != z)
+        def _(s=s):
+            grad_copy(s, 0).wait_send()
+            pltpu.make_async_remote_copy(
+                src_ref=gate_grads_sent.at[s],
+                dst_ref=gate_grads.at[s],
+                send_sem=grad_send.at[s],
+                recv_sem=grad_recv.at[s],
+                device_id=(dp, z),
+                device_id_type=MESH,
+            ).wait_recv()
+
+    last = (
+        pltpu.make_async_copy(rows, rows_all_hbm, local_sem.at[0]),
+        pltpu.make_async_copy(gate_grads, gate_grads_hbm, local_sem.at[1]),
+    )
+    for copy in last:
+        copy.start()
+    for copy in last:
+        copy.wait()
+
+
+def front(
+    late,
+    tokens,
+    cots,
+    gain_rows,
+    heads_in,
+    heads_out,
+    router_rows,
+    route_rows,
+    tables,
+    up,
+    down,
+    line,
+    prompt,
+):
     count, width = tokens.shape
-    experts = router_rows.shape[0]
+    named = router_rows.shape[0]
+    experts, _, ff_width = down.shape
     kv_width = KV_HEADS * HEAD_DIM
     shape = jax.ShapeDtypeStruct
+    padded = experts + -experts % 8
     held = pl.BlockSpec(memory_space=pltpu.VMEM)
     anywhere = pl.BlockSpec(memory_space=pl.ANY)
+    small = pltpu.VMEM((line, padded, count), F32)
     return pl.pallas_call(
-        functools.partial(attend_kernel, line),
+        functools.partial(front_kernel, line, prompt, late),
         out_shape=(
             shape((count, width), BF16),
             shape((count, HEADS * HEAD_DIM), BF16),
@@ -820,22 +863,64 @@
             shape((count, HEADS * HEAD_DIM), BF16),
             shape((count, width), F32),
             shape((count, width), BF16),
-            shape((experts, count), F32),
+            shape((named, count), F32),
             shape((count, 128), F32),
             shape((line, count, width), BF16),
+            shape((line, count, width), BF16),
+            shape((2, count, width), BF16),
+            shape((line, count, width), BF16),
+            shape((line, padded, count), F32),
+            shape((line, count, experts * ff_width), BF16),
+            shape((line, count, experts * 2 * ff_width), BF16),
+            shape((line, count, width), BF16),
         ),
-        in_specs=[held, anywhere] + [held] * 8,
-        out_specs=(held,) * 9 + (anywhere,),
+        in_specs=[held, anywhere] + [held] * 8 + [anywhere] * 2,
+        out_specs=(held,) * 9 + (anywhere,) * 8,
         scratch_shapes=[
+            pltpu.VMEM((count, width), BF16),
+            pltpu.VMEM((line, count, width), BF16),
+            small,
+            small,
+            small,
+            small,
+            pltpu.VMEM((width, experts * 2 * ff_width), BF16),
+            pltpu.VMEM((width, experts * ff_width), BF16),
+            pltpu.VMEM((count, heads_in.shape[1]), F32),
+            pltpu.VMEM((2, count, width), BF16),
+            pltpu.VMEM((line, count, width), BF16),
+            pltpu.VMEM((2, count, experts * ff_width), BF16),
+            pltpu.VMEM((2, count, experts * 2 * ff_width), BF16),
+            pltpu.VMEM((count, 128), F32),
             pltpu.SemaphoreType.DMA((line + 2,)),
             pltpu.SemaphoreType.DMA((line,)),
-            pltpu.SemaphoreType.DMA,
+            pltpu.SemaphoreType.DMA((line + 2,)),
+            pltpu.SemaphoreType.DMA((line,)),
+            pltpu.SemaphoreType.DMA((line,)),
+            pltpu.SemaphoreType.DMA((line,)),
+            pltpu.SemaphoreType.DMA((2, experts)),
+            pltpu.SemaphoreType.DMA((6,)),
+            pltpu.SemaphoreType.DMA((2, 3)),
+            pltpu.SemaphoreType.DMA((line,)),
+            pltpu.SemaphoreType.DMA((line,)),
+            pltpu.SemaphoreType.DMA((line,)),
+            pltpu.SemaphoreType.DMA((line,)),
         ],
         compiler_params=pltpu.CompilerParams(
             collective_id=4, has_side_effects=True, vmem_limit_bytes=VMEM_MOST
         ),
-        cost_estimate=pl.CostEstimate(flops=2**33, bytes_accessed=2**24, transcendentals=2**21),
-    )(tokens, cots, gain_rows, heads_in, heads_out, router_rows, route_rows, *tables)
+        cost_estimate=pl.CostEstimate(flops=2**35, bytes_accessed=2**26, transcendentals=2**22),
+    )(
+        tokens,
+        cots,
+        gain_rows,
+        heads_in,
+        heads_out,
+        router_rows,
+        route_rows,
+        *tables,
+        up,
+        down,
+    )
 
 
 def attend_back_kernel(
@@ -861,20 +946,26 @@
     tokens_hbm,
     first_hbm,
     in_hbm,
-    token_grad,
-    sum_hbm,
-    small_hbm,
-    tokens,
-    first_in,
-    heads_in,
-    grad_hidden,
-    grad_attended,
-    grad_projected,
-    small_rows,
-    own,
-    own_small,
-    *scratch,
+    mix_hbm,
+    late_hbm,
+    *others,
 ):
+    bank_hbm, others = (others[0], others[1:]) if paired else (None, others)
+    output, token_grad, sum_hbm, small_hbm, *others = others
+    bank_sum_hbm, others = (others[0], others[1:]) if paired else (None, others)
+    (
+        tokens,
+        first_in,
+        heads_in,
+        mixes,
+        grad_hidden,
+        grad_attended,
+        grad_projected,
+        small_rows,
+        own,
+        own_small,
+        *scratch,
+    ) = others
     dp = lax.axis_index("dp")
     z = lax.axis_index("expert")
     units = own.shape[0]
@@ -887,6 +978,20 @@
     )
     for copy in loads:
         copy.start()
+
+    def mix_load(b):
+        return pltpu.make_async_copy(mix_hbm.at[b], mixes.at[b], load_sem.at[5 + b])
+
+    def direct(b):
+        ends = (z == 0) | (z == line - 1)
+        return jnp.logical_not(ends) | (z == b) if paired else z == z
+
+    for b in range(line):
+
+        @pl.when(direct(b))
+        def _(b=b):
+            mix_load(b).start()
+
     if paired:
         (
             cores,
@@ -906,6 +1011,12 @@
             line_send,
             line_recv,
             out_sem,
+            bank_kept,
+            bank_last,
+            bank_total,
+            bank_sem,
+            late_send_sem,
+            late_recv_sem,
         ) = scratch[1:]
         rows = totals.shape[1]
         y, x, core = dp // 4, lax.rem(dp // 2, 2), lax.rem(dp, 2)
@@ -918,6 +1029,49 @@
                 barrier, inc=1, device_id=(dp, lax.rem(z + step, line)), device_id_type=MESH
             )
         pl.semaphore_wait(barrier, 3 + line - 1)
+
+        def bank_kept_copy(e):
+            kept = y if e % 2 == 0 else x
+            return pltpu.make_async_copy(
+                bank_hbm.at[e, kept], bank_kept.at[e], bank_sem.at[0, e]
+            )
+
+        def bank_last_copy(e):
+            sent, peer = (1 - y, y_peer) if e % 2 == 0 else (1 - x, x_peer)
+            return pltpu.make_async_remote_copy(
+                src_ref=bank_hbm.at[e, sent],
+                dst_ref=bank_last.at[e],
+                send_sem=bank_sem.at[1, e],
+                recv_sem=bank_sem.at[2, e],
+                device_id=(peer, z),
+                device_id_type=MESH,
+            )
+
+        def bank_total_copy(e):
+            return pltpu.make_async_copy(
+                bank_total.at[e], bank_sum_hbm.at[e], bank_sem.at[3, e]
+            )
+
+        for e in range(bank_hbm.shape[0]):
+            bank_kept_copy(e).start()
+            bank_last_copy(e).start()
+
+        def late_send(side, source):
+            return pltpu.make_async_remote_copy(
+                src_ref=late_hbm.at[side],
+                dst_ref=mixes.at[source],
+                send_sem=late_send_sem.at[side],
+                recv_sem=late_recv_sem.at[source],
+                device_id=(dp, side * (line - 1)),
+                device_id_type=MESH,
+            )
+
+        for side in range(2):
+
+            @pl.when(z != side * (line - 1))
+            def _(side=side):
+                late_send(side, z).start()
+
         buffers = (own, cores, firsts, lasts, sums, lines, totals)
         small_buffers = (
             own_small,
@@ -1129,15 +1283,10 @@
         if paired:
             wide_sums.core_send(2 + j).start()
             wide_sums.after_core(1 + j)
-            wide_sums.after_first(j)
-
-            @pl.when(j >= 1)
-            def _():
-                wide_sums.after_last(j - 1)
 
             @pl.when(j >= 2)
             def _():
-                wide_sums.after_line(j - 2)
+                wide_sums.after_first(j - 2)
 
         return 0
 
@@ -1146,8 +1295,8 @@
     last = units - 1
     if paired:
         wide_sums.after_core(last)
-        wide_sums.after_first(last - 1)
-        wide_sums.after_last(last - 2)
+        wide_sums.after_first(2)
+        wide_sums.after_last(0)
     loads[1].wait()
     loads[2].wait()
     grad_first = jnp.zeros(grad_hidden.shape, F32)
@@ -1169,16 +1318,36 @@
         small_sum.core_send(0).start()
     token_grad[...] = grad_hidden[...] + norm_grad
     if paired:
-        wide_sums.after_line(last - 3)
+        for e in range(bank_hbm.shape[0]):
+            bank_kept_copy(e).wait()
+            bank_last_copy(e).wait()
+            bank_total[e] = bank_kept[e].astype(F32) + bank_last[e].astype(F32)
+            bank_total_copy(e).start()
+
+    @pl.when(direct(-1))
+    def _():
+        total = hidden[...]
+        for b in range(line):
+            mix_load(b).wait()
+            total = total + mixes[b].astype(F32)
+        output[...] = total.astype(BF16)
+
+    if paired:
         small_sum.after_core(0)
-        wide_sums.after_first(last)
-        wide_sums.after_last(last - 1)
-        wide_sums.after_line(last - 2)
+        wide_sums.after_first(3)
+        wide_sums.after_last(1)
+        wide_sums.after_first(4)
+        wide_sums.after_last(2)
         small_sum.after_first(0)
-        wide_sums.after_last(last)
+        wide_sums.after_first(5)
+        wide_sums.after_last(3)
         small_sum.after_last(0)
-        wide_sums.after_line(last - 1)
-        wide_sums.after_line(last)
+        wide_sums.after_line(0)
+        wide_sums.after_last(4)
+        wide_sums.after_line(1)
+        wide_sums.after_last(5)
+        for u in range(2, units):
+            wide_sums.after_line(u)
         small_sum.after_line(0)
         outs = (
             pltpu.make_async_copy(totals, sum_hbm, out_sem.at[0]),
@@ -1195,12 +1364,30 @@
         for u in range(units):
             wide_sums.finish(u)
         small_sum.finish(0)
+        for e in range(bank_hbm.shape[0]):
+            bank_total_copy(e).wait()
+        for side in range(2):
+
+            @pl.when(z != side * (line - 1))
+            def _(side=side):
+                late_send(side, z).wait_send()
+
+            @pl.when(z == side * (line - 1))
+            def _():
+                mix_load(z).wait()
+                total = hidden[...] + mixes[z].astype(F32)
+                for step in range(1, line):
+                    source = lax.rem(z + step, line)
+                    late_send(0, source).wait_recv()
+                    total = total + mixes[source].astype(F32)
+                output[...] = total.astype(BF16)
+
     for copy in outs:
         copy.wait()
 
 
 def attend_back(held_args, far_args, paired, line):
-    tokens, first_in, heads_in = far_args
+    tokens, first_in, heads_in = far_args[:3]
     count, width = tokens.shape
     pairs = KV_HEADS // 2
     units = 2 + pairs
@@ -1234,25 +1421,36 @@
             pltpu.SemaphoreType.DMA((units + 1, line)),
             pltpu.SemaphoreType.DMA((2,)),
         ]
+        bank_shape = (far_args[5].shape[0],) + far_args[5].shape[2:]
+        sum_shapes += (shape(bank_shape, F32),)
+        exchange += [
+            pltpu.VMEM(bank_shape, BF16),
+            pltpu.VMEM(bank_shape, BF16),
+            pltpu.VMEM(bank_shape, F32),
+            pltpu.SemaphoreType.DMA((4, bank_shape[0])),
+            pltpu.SemaphoreType.DMA((2,)),
+            pltpu.SemaphoreType.DMA((line,)),
+        ]
     settings = dict(vmem_limit_bytes=VMEM_MOST)
     if paired:
         settings.update(collective_id=3, has_side_effects=True)
     return pl.pallas_call(
         functools.partial(attend_back_kernel, paired, line),
-        out_shape=(shape((count, width), F32),) + sum_shapes,
-        in_specs=[held] * len(held_args) + [anywhere] * 3,
-        out_specs=(held, anywhere, anywhere),
+        out_shape=(shape((count, width), BF16), shape((count, width), F32)) + sum_shapes,
+        in_specs=[held] * len(held_args) + [anywhere] * len(far_args),
+        out_specs=(held, held) + (anywhere,) * len(sum_shapes),
         scratch_shapes=[
             pltpu.VMEM((count, width), BF16),
             pltpu.VMEM((count, width), BF16),
             pltpu.VMEM(heads_in.shape, BF16),
+            pltpu.VMEM((line, count, width), BF16),
             pltpu.VMEM((count, width), F32),
             pltpu.VMEM((count, HEADS * HEAD_DIM), BF16),
             pltpu.VMEM((pairs, count, 4 * PAIR), BF16),
             pltpu.VMEM((128, width), F32),
             pltpu.VMEM((units, 2, 2, 2, block_rows, UNIT), BF16),
             pltpu.VMEM((1, 2, 2, 2, block_rows, 128), BF16),
-            pltpu.SemaphoreType.DMA((5,)),
+            pltpu.SemaphoreType.DMA((5 + line,)),
             *exchange,
         ],
         compiler_params=pltpu.CompilerParams(**settings),
@@ -1330,7 +1528,15 @@
         gates,
         log_totals,
         cots_all,
-    ) = attend(
+        mix_all,
+        mix_late,
+        grad_part,
+        gate_grads,
+        gated,
+        grad_gate_up,
+        rows_all,
+    ) = front(
+        paired,
         tokens,
         cotangent,
         gain_rows,
@@ -1339,14 +1545,10 @@
         router_rows,
         routes.T,
         tables,
+        expert_in,
+        expert_out,
         peer_count,
-    )
-    padded = -local_experts % 8
-    gate_rows = jnp.pad(
-        gates.reshape(peer_count, local_experts, token_count), ((0, 0), (0, padded), (0, 0))
-    )
-    mix_part, grad_part, gate_grads, gated, grad_gate_up, rows_all = bank(
-        second_in, cots_all, gate_rows, expert_in, expert_out, peer_count
+        token_count - cont_ids.shape[1],
     )
     back_rows = lax.psum_scatter(
         grad_part.reshape(peer_count * token_count, model_width),
@@ -1361,24 +1563,13 @@
         grad_gate_up.reshape(peer_count * token_count, -1),
     )
     if paired:
-        bank_sums = bank_grads(*grad_sources, local_experts)
-        expert_sums = (bank_sums[:, :, : expert_in.shape[2]], bank_sums[:, :, expert_in.shape[2] :])
+        expert_sums = (bank_grads(*grad_sources, local_experts),)
     else:
         expert_sums = tuple(
             lax.psum_scatter(part, "dp", scatter_dimension=1, tiled=True).astype(jnp.float32)
             for part in weight_grads(*grad_sources, local_experts)
         )
-    mix_part, back_rows, expert_sums = lax.optimization_barrier(
-        (mix_part, back_rows, expert_sums)
-    )
-    mixture = lax.psum_scatter(
-        mix_part.reshape(peer_count * token_count, model_width),
-        "expert",
-        scatter_dimension=0,
-        tiled=True,
-    ).astype(jnp.float32)
-    output = (hidden + mixture).astype(jnp.bfloat16)
-    token_grad, unit_sums, small_sum = attend_back(
+    output, token_grad, unit_sums, small_sum, *bank_sums = attend_back(
         (
             back_rows,
             hidden,
@@ -1396,12 +1587,14 @@
             log_totals,
             *tables,
         ),
-        (tokens, first_in, heads_in),
+        (tokens, first_in, heads_in, mix_all, mix_late, *(expert_sums if paired else ())),
         paired,
         peer_count,
     )
     if paired:
         small_sum = small_sum[0]
+        cut = expert_in.shape[2]
+        expert_sums = (bank_sums[0][:, :, :cut], bank_sums[0][:, :, cut:])
     else:
         head_parts = unit_columns(unit_sums.reshape(unit_sums.shape[0], model_width, UNIT))
         packed = jnp.concatenate([*head_parts, small_sum.reshape(model_width, 128)], axis=1)
@@ -1418,17 +1611,22 @@
     summed = (
         head_in_sum,
         head_out_sum,
-        small_sum[:, :experts],
-        small_sum[:, experts : experts + 2],
     )
     shard_rows = model_width // lax.axis_size(("dp", "expert"))
+    small_rows = small_sum.T
     gains_share = lax.dynamic_slice_in_dim(
-        norm_gains, lax.axis_index(("dp", "expert")) * shard_rows, shard_rows, 0
-    )
-    gains_new = update(summed[3], gains_share, gains_moment, gains_average)
+        gain_rows, lax.axis_index(("dp", "expert")) * shard_rows, shard_rows, 1
+    )
+    gains_new = update(
+        small_rows[experts : experts + 2], gains_share, gains_moment.T, gains_average.T
+    )
+    gains_new = tuple(value.T for value in gains_new)
     inproj_new = update(summed[0], heads_in_master, heads_in_moment, heads_in_average)
     outproj_new = update(summed[1], heads_out_master, heads_out_moment, heads_out_average)
-    router_new = update(summed[2], router_master, router_moment, router_average)
+    router_new = update(
+        small_rows[:experts], router_master.T, router_moment.T, router_average.T
+    )
+    router_new = tuple(value.T for value in router_new)
     upper_new = update(expert_sums[0], expert_in_master, expert_in_moment, expert_in_average)
     lower_new = update(expert_sums[1], expert_out_master, expert_out_moment, expert_out_average)
     return (

time: 349 us -> 311 us (0.89)
  Pallas kernels: 298 us -> 267 us
  local copies, waits for them, and re-layouts: 16.6 us -> 12.2 us
    pallas_call x2 -> x1, Pallas kernels: 153 us -> 132 us  [front(): pl.pallas_call(functools.partial(front_kernel, line, prompt, late), out_s...]
    pallas_call x1, Pallas kernels: 76.4 us -> 58.2 us  [bank_grads(): pl.pallas_call(bank_grads_kernel, out_shape=jax.ShapeDtypeStruct((experts...]
    pallas_call x1, Pallas kernels: 68.3 us -> 76.3 us  [attend_back(): pl.pallas_call(functools.partial(attend_back_kernel, paired, line), out_s...]
    unnamed x50 -> x53, local copies, waits for them, and re-layouts: 12.9 us -> 9.93 us
    add x6 -> x4, other arithmetic: 12.6 us -> 12.2 us  [update(): DECAY * average + (1.0 - DECAY) * master_next]
  transfers between devices with their start and end apart: 2 -> 1, of which waited for: 0 -> 0; matrix products, arithmetic and copies ran while one was open for 7% -> 1% of each run, Pallas kernels for 42% -> 19%
where the time goes in v1:
time: 311 us
  Pallas kernels  267 us (86%)
  other arithmetic  17.5 us (6%)
  between operations  14.3 us (5%)
  local copies, waits for them, and re-layouts  12.2 us (4%)
    pallas_call x1, Pallas kernels, front(): pl.pallas_call(functools.partial(front_kernel, line, prompt, late), out_s...  132 us
    pallas_call x1, Pallas kernels, attend_back(): pl.pallas_call(functools.partial(attend_back_kernel, paired, line), out_s...  76.3 us
    pallas_call x1, Pallas kernels, bank_grads(): pl.pallas_call(bank_grads_kernel, out_shape=jax.ShapeDtypeStruct((experts...  58.2 us
    add x4, other arithmetic, update(): DECAY * average + (1.0 - DECAY) * master_next  12.2 us
    unnamed x53, local copies, waits for them, and re-layouts  9.93 us
  transfers between devices with their start and end apart: 1, of which 0 were waited for; matrix products, arithmetic and copies ran while one was open for 1% of the time, Pallas kernels for 19%

profile of v1, /device:TPU:0, one launch (start us, length us, event | category | flops | bytes accessed | tf_op | source)
XLA Modules:
  0.0 310.9 jit_solution(15052117112139736475)
XLA Ops:
  7.2 0.0 reduce-scatter.2.cloned.1.call-start
  7.3 0.9 convert_reduce_fusion
  8.2 0.7 concatenate.22
  8.9 0.8 fusion.2
  9.6 1.0 fusion.1.bias
  10.6 1.1 pad_maximum_fusion
  11.7 132.3 %shard_map.410 = (bf16[384,1024]{1,0:T(8,128)(2,1)}, bf16[384,1024]{1,0:T(8,128)(2,1)}, bf16[384,512]{1,0:T(8,128)(2,1)}, bf16[384,512]{1,0:T(8,128)(2,1)}, bf16...) custom-call(bf16[384,1024]{1,0:T(8,128)(2,1)} %tokens_hbm.1, ...), custom_call_target="tpu_custom_call" | custom-call | flops 34359738368 | bytes 67108864 | tf_op jit(solution)/shard_map/pallas_call | solution.py:856
  144.0 0.0 copy-start.12
  144.0 0.0 copy-start.16
  144.0 0.0 copy-start.17
  144.0 0.0 copy-start.13
  144.1 0.0 copy-start.14
  144.1 0.0 copy-start.15
  144.1 0.0 reduce-scatter.2.cloned.1.call-update
  144.1 0.7 copy-done.12
  144.8 0.6 reshape.99.gate_grads
  145.4 0.0 copy-done.16
  145.4 0.1 copy.100
  145.5 0.0 copy-done.17
  145.5 0.1 copy.99
  145.6 0.8 constant_dynamic-slice_fusion
  146.4 0.1 copy.116
  146.5 0.0 copy-done.13
  146.5 0.1 copy.108
  146.6 0.0 copy-done.14
  146.6 0.1 copy.106
  146.6 0.0 copy-done.15
  146.6 0.1 copy.105
  146.7 58.2 %shard_map.411.others_0_ = bf16[4,2,128,1536]{3,2,1,0:T(8,128)(2,1)} custom-call(bf16[1536,1024]{1,0:T(8,128)(2,1)} %bitcast.97, bf16[1536,1024]{1,0:T(8,128)(2,1)} %bitcast.96, bf16[1536,2048]{1,0:T(8,128)(2,1)} %bitcast.95, bf16[1536,4096]{1,0:T(8,128)(2,1)} %bitcast.94), custom_call_target="tpu_custom_call" | custom-call | flops 19327352832 | bytes 134217728 | tf_op jit(solution)/shard_map/pallas_call | solution.py:342
  205.0 0.0 reduce-scatter.2.cloned.1.call-done.back_rows
  205.0 76.3 %shard_map.412 = (bf16[384,1024]{1,0:T(8,128)(2,1)}, f32[384,1024]{1,0:T(8,128)}, f32[6,32,512]{2,1,0:T(8,128)}, f32[1,32,128]{2,1,0:T(8,128)}, f32[4,128,1536]{2,1,0:T(8,128)}) custom-call(bf16[384,1024]{1,0:T(8,128)(2,1)} %reduce-scatter.2.cloned.1.call-done.back_rows, f32[384,1024]{1,0:T(8,128)} %get-tuple-element.43.hidden, bf16[384,1024]{1,0:T(8,128)(2,1)} %cots.1, ...), custom_call_target="tpu_custom_call" | custom-call | flops 17179869184 | bytes 33554432 | tf_op jit(solution)/shard_map/pallas_call | solution.py:1437
  281.3 0.0 copy-start
  281.3 1.1 slice_bitcast_fusion.1
  282.4 0.9 slice_bitcast_fusion.2
  283.3 0.9 slice_bitcast_fusion
  284.2 0.8 fusion.4
  285.0 0.6 copy.110
  285.6 0.6 copy.111
  286.3 0.6 copy.112
  287.0 0.7 fusion.3
  287.7 0.7 copy.113
  288.4 0.7 copy.114
  289.0 0.7 copy.115
  289.7 0.0 copy-done
  289.7 0.0 copy-start.2
  289.7 0.0 copy-start.3
  289.8 0.0 copy-start.4
  289.8 7.0 %multiply_add_fusion = (f32[4,128,1024]{2,1,0:T(8,128)}, f32[4,128,1024]{2,1,0:T(8,128)}, f32[4,128,1024]{2,1,0:T(8,128)}) fusion(f32[4,128,1024]{2,1,0:T(8,128)S(1)} %copy-done, f32[4,128,1024]{2,1,0:T(8,128)} %param.47, f32[4,128,1536]{2,1,0:T(8,128)} %get-tuple-element.63, f32[4,128,1024]{2,1,0:T(8,128)} %param.48), kind=kLoop, calls=%fused_computation | loop fusion | flops 4718592 | bytes 14680064 | tf_op jit(solution)/shard_map/add | solution.py:50
  296.8 0.0 copy-done.2
  296.8 0.0 copy-done.3
  296.8 0.0 copy-done.4
  296.8 0.0 copy-start.6
  296.8 0.0 copy-start.7
  296.8 0.0 copy-start.8
  296.8 0.0 copy-start.9
  296.8 0.0 copy-start.10
  296.8 0.0 copy-start.11
  296.9 3.4 %multiply_add_fusion.2 = (f32[4,128,512]{2,1,0:T(8,128)}, f32[4,128,512]{2,1,0:T(8,128)}, f32[4,128,512]{2,1,0:T(8,128)}) fusion(f32[4,128,512]{2,1,0:T(8,128)S(1)} %copy-done.2, f32[4,128,512]{2,1,0:T(8,128)S(1)} %copy-done.3, f32[4,128,1536]{2,1,0:T(8,128)} %get-tuple-element.63, f32[4,128,512]{2,1,0:T(8,128)S(1)} %copy-done.4), kind=kLoop, calls=%fused_computation.3 | loop fusion | flops 2359296 | bytes 7340032 | tf_op jit(solution)/shard_map/add | solution.py:50
  300.3 0.0 copy-done.7
  300.3 1.0 multiply_add_fusion.4
  301.3 0.0 copy-done.11
  301.3 0.8 multiply_add_fusion.6
  302.1 0.9 copy.127
  303.0 1.1 copy.128
  (23 shorter events, 0.1 us)
Async XLA Ops:
  7.2 197.8 %reduce-scatter.2.cloned.1.call-start = ((), (), s32[]{:S(2)}) async-start(), calls=%async_computation.1 | async-start | bytes 3932160 | tf_op jit(solution)/shard_map/reduce_scatter | solution.py:1553
  144.0 0.8 copy-start.12
  144.0 1.4 copy-start.16
  144.0 1.5 copy-start.17
  144.0 2.4 copy-start.13
  144.1 2.5 copy-start.14
  144.1 2.6 copy-start.15
  281.3 8.4 %copy-start = (f32[4,128,1024]{2,1,0:T(8,128)S(1)}, f32[4,128,1024]{2,1,0:T(8,128)}, u32[]{:S(2)}) copy-start(f32[4,128,1024]{2,1,0:T(8,128)} %param.49) | copy-start | bytes 6291460
  289.7 7.0 %copy-start.2 = (f32[4,128,512]{2,1,0:T(8,128)S(1)}, f32[4,128,512]{2,1,0:T(8,128)}, u32[]{:S(2)}) copy-start(f32[4,128,512]{2,1,0:T(8,128)} %param.53) | copy-start | bytes 3145732
  289.7 7.0 %copy-start.3 = (f32[4,128,512]{2,1,0:T(8,128)S(1)}, f32[4,128,512]{2,1,0:T(8,128)}, u32[]{:S(2)}) copy-start(f32[4,128,512]{2,1,0:T(8,128)} %param.51) | copy-start | bytes 3145732
  289.8 7.0 %copy-start.4 = (f32[4,128,512]{2,1,0:T(8,128)S(1)}, f32[4,128,512]{2,1,0:T(8,128)}, u32[]{:S(2)}) copy-start(f32[4,128,512]{2,1,0:T(8,128)} %param.52) | copy-start | bytes 3145732
  296.8 3.5 %copy-start.6 = (f32[32,2048]{1,0:T(8,128)S(1)}, f32[32,2048]{1,0:T(8,128)}, u32[]{:S(2)}) copy-start(f32[32,2048]{1,0:T(8,128)} %param.37) | copy-start | bytes 786436
  296.8 3.5 %copy-start.7 = (f32[32,2048]{1,0:T(8,128)S(1)}, f32[32,2048]{1,0:T(8,128)}, u32[]{:S(2)}) copy-start(f32[32,2048]{1,0:T(8,128)} %param.35) | copy-start | bytes 786436
  296.8 3.5 %copy-start.8 = (f32[32,2048]{1,0:T(8,128)S(1)}, f32[32,2048]{1,0:T(8,128)}, u32[]{:S(2)}) copy-start(f32[32,2048]{1,0:T(8,128)} %param.36) | copy-start | bytes 786436
  296.8 4.5 %copy-start.9 = (f32[32,1024]{1,0:T(8,128)S(1)}, f32[32,1024]{1,0:T(8,128)}, u32[]{:S(2)}) copy-start(f32[32,1024]{1,0:T(8,128)} %param.41) | copy-start | bytes 393220
  296.8 4.5 %copy-start.10 = (f32[32,1024]{1,0:T(8,128)S(1)}, f32[32,1024]{1,0:T(8,128)}, u32[]{:S(2)}) copy-start(f32[32,1024]{1,0:T(8,128)} %param.39) | copy-start | bytes 393220
  296.8 4.4 %copy-start.11 = (f32[32,1024]{1,0:T(8,128)S(1)}, f32[32,1024]{1,0:T(8,128)}, u32[]{:S(2)}) copy-start(f32[32,1024]{1,0:T(8,128)} %param.40) | copy-start | bytes 393220
  300.3 1.8 copy-start.5
  300.3 2.7 copy-start.1
Sparse Core Ops, SparseCore 0:
  144.2 60.5 reduce-scatter.1

commit v2 on v1

--- a/solution.py
+++ b/solution.py
@@ -370,6 +370,7 @@
 
 PAIR = 2 * HEAD_DIM
 UNIT = 512
+PIECES = 3
 
 
 def swap_halves(value):
@@ -406,8 +407,8 @@
     tokens,
     cots_hbm,
     gain_rows,
-    heads_in,
-    heads_out,
+    heads_in_hbm,
+    heads_out_hbm,
     router_rows,
     route_rows,
     cosine,
@@ -415,13 +416,13 @@
     bias,
     up_hbm,
     down_hbm,
-    first_in,
-    queries,
-    keys,
-    values,
-    attended,
-    hidden,
-    second_in,
+    first_in_hbm,
+    queries_hbm,
+    keys_hbm,
+    values_hbm,
+    attended_hbm,
+    hidden_hbm,
+    second_in_hbm,
     gate_rows,
     log_totals,
     cots_all,
@@ -459,6 +460,16 @@
     grad_recv,
     mix_send,
     mix_recv,
+    heads_in,
+    heads_out,
+    first_in,
+    queries,
+    keys,
+    values,
+    attended,
+    hidden,
+    second_in,
+    held_sem,
 ):
     dp = lax.axis_index("dp")
     z = lax.axis_index("expert")
@@ -469,6 +480,23 @@
     start_rows, pass_rows, finish_rows = line_gather(
         line, z, dp, second_in, rows, row_send, row_recv
     )
+
+    heads_in_load = pltpu.make_async_copy(heads_in_hbm, heads_in, held_sem.at[0])
+    heads_out_load = pltpu.make_async_copy(heads_out_hbm, heads_out, held_sem.at[1])
+    held_out = [
+        pltpu.make_async_copy(source, target, held_sem.at[2 + number])
+        for number, (source, target) in enumerate(
+            (
+                (first_in, first_in_hbm),
+                (queries, queries_hbm),
+                (keys, keys_hbm),
+                (values, values_hbm),
+                (attended, attended_hbm),
+                (hidden, hidden_hbm),
+                (second_in, second_in_hbm),
+            )
+        )
+    ]
 
     def weight_copies(e):
         return (
@@ -493,6 +521,8 @@
     start_cots()
     cots_in = pltpu.make_async_copy(cots_hbm, cots, local_sem.at[2])
     cots_in.start()
+    heads_in_load.start()
+    heads_out_load.start()
     for e in range(experts):
         for copy in weight_copies(e):
             copy.start()
@@ -506,6 +536,8 @@
     cots_in.wait()
     own_cots = pltpu.make_async_copy(cots, cots_all.at[z], local_sem.at[0])
     own_cots.start()
+
+    heads_in_load.wait()
 
     def project(i, _):
         at = lanes_at(i * UNIT, UNIT)
@@ -563,12 +595,15 @@
         return 0
 
     lax.fori_loop(0, KV_HEADS // 2, pair, 0)
+    heads_out_load.wait()
     hidden_rows = token_rows + contract(attended[...], heads_out[...], 1, 1)
     hidden[...] = hidden_rows
     factor = lax.rsqrt(jnp.mean(hidden_rows * hidden_rows, axis=1, keepdims=True) + EPS)
     second = (hidden_rows * factor * gain_rows[1:2]).astype(BF16)
     second_in[...] = second
     start_rows()
+    for copy in held_out:
+        copy.start()
     own_rows = pltpu.make_async_copy(second_in, rows.at[z], local_sem.at[1])
     own_rows.start()
     logits = contract(router_rows[...], second, 1, 1)
@@ -781,6 +816,8 @@
 
     finish_rows()
     finish_cots()
+    for copy in held_out:
+        copy.wait()
     own_mix().wait()
     if late:
         for side in range(2):
@@ -874,8 +911,8 @@
             shape((line, count, experts * 2 * ff_width), BF16),
             shape((line, count, width), BF16),
         ),
-        in_specs=[held, anywhere] + [held] * 8 + [anywhere] * 2,
-        out_specs=(held,) * 9 + (anywhere,) * 8,
+        in_specs=[held, anywhere, held, anywhere, anywhere] + [held] * 5 + [anywhere] * 2,
+        out_specs=(anywhere,) * 7 + (held,) * 2 + (anywhere,) * 8,
         scratch_shapes=[
             pltpu.VMEM((count, width), BF16),
             pltpu.VMEM((line, count, width), BF16),
@@ -904,6 +941,16 @@
             pltpu.SemaphoreType.DMA((line,)),
             pltpu.SemaphoreType.DMA((line,)),
             pltpu.SemaphoreType.DMA((line,)),
+            pltpu.VMEM(heads_in.shape, BF16),
+            pltpu.VMEM(heads_out.shape, BF16),
+            pltpu.VMEM((count, width), BF16),
+            pltpu.VMEM((count, HEADS * HEAD_DIM), BF16),
+            pltpu.VMEM((count, kv_width), BF16),
+            pltpu.VMEM((count, kv_width), BF16),
+            pltpu.VMEM((count, HEADS * HEAD_DIM), BF16),
+            pltpu.VMEM((count, width), F32),
+            pltpu.VMEM((count, width), BF16),
+            pltpu.SemaphoreType.DMA((9,)),
         ],
         compiler_params=pltpu.CompilerParams(
             collective_id=4, has_side_effects=True, vmem_limit_bytes=VMEM_MOST
@@ -1015,8 +1062,12 @@
             bank_last,
             bank_total,
             bank_sem,
-            late_send_sem,
-            late_recv_sem,
+            small_columns,
+            chain_own,
+            chain_in,
+            chain_out,
+            chain_load_sem,
+            chain_sem,
         ) = scratch[1:]
         rows = totals.shape[1]
         y, x, core = dp // 4, lax.rem(dp // 2, 2), lax.rem(dp, 2)
@@ -1056,21 +1107,58 @@
             bank_kept_copy(e).start()
             bank_last_copy(e).start()
 
-        def late_send(side, source):
+        piece = hidden.shape[0] // PIECES
+
+        def part(p):
+            return pl.ds(p * piece, piece)
+
+        def chain_load(side):
+            return pltpu.make_async_copy(
+                late_hbm.at[side], chain_own.at[side], chain_load_sem.at[side]
+            )
+
+        def chain_send(side, p, source):
             return pltpu.make_async_remote_copy(
-                src_ref=late_hbm.at[side],
-                dst_ref=mixes.at[source],
-                send_sem=late_send_sem.at[side],
-                recv_sem=late_recv_sem.at[source],
-                device_id=(dp, side * (line - 1)),
+                src_ref=source.at[side, part(p)],
+                dst_ref=chain_in.at[side, part(p)],
+                send_sem=chain_sem.at[0, side, p],
+                recv_sem=chain_sem.at[1, side, p],
+                device_id=(dp, jnp.clip(z + 2 * side - 1, 0, line - 1)),
                 device_id_type=MESH,
             )
 
+        inside = (z > 0) & (z < line - 1)
+        starts = (z == line - 1, z == 0)
         for side in range(2):
 
-            @pl.when(z != side * (line - 1))
+            @pl.when(inside)
             def _(side=side):
-                late_send(side, z).start()
+                chain_load(side).start()
+
+            @pl.when(starts[side])
+            def _(side=side):
+                for p in range(PIECES):
+                    chain_send(side, p, late_hbm).start()
+
+        def relay(side, p):
+            if p == 0:
+                chain_load(side).wait()
+            chain_send(side, p, chain_out).wait_recv()
+            chain_out[side, part(p)] = (
+                chain_own[side, part(p)].astype(F32) + chain_in[side, part(p)].astype(F32)
+            ).astype(BF16)
+            chain_send(side, p, chain_out).start()
+
+        def relay_on(near, p):
+            low_half = 2 * z < line - 1
+
+            @pl.when(inside & low_half)
+            def _():
+                relay(1 if near else 0, p)
+
+            @pl.when(inside & jnp.logical_not(low_half))
+            def _():
+                relay(0 if near else 1, p)
 
         buffers = (own, cores, firsts, lasts, sums, lines, totals)
         small_buffers = (
@@ -1237,6 +1325,7 @@
     loads[0].wait()
     if paired:
         wide_sums.after_core(0)
+        relay_on(True, 0)
 
     def pair(j, _):
         key_pair = keys[:, lanes_at(j * PAIR, PAIR)]
@@ -1288,6 +1377,12 @@
             def _():
                 wide_sums.after_first(j - 2)
 
+            for at, near, p in ((0, True, 1), (1, True, 2), (2, False, 0), (3, False, 1)):
+
+                @pl.when(j == at)
+                def _(near=near, p=p):
+                    relay_on(near, p)
+
         return 0
 
     pairs = KV_HEADS // 2
@@ -1295,6 +1390,7 @@
     last = units - 1
     if paired:
         wide_sums.after_core(last)
+        relay_on(False, 2)
         wide_sums.after_first(2)
         wide_sums.after_last(0)
     loads[1].wait()
@@ -1349,10 +1445,21 @@
         for u in range(2, units):
             wide_sums.after_line(u)
         small_sum.after_line(0)
-        outs = (
-            pltpu.make_async_copy(totals, sum_hbm, out_sem.at[0]),
-            pltpu.make_async_copy(small_totals, small_hbm, out_sem.at[1]),
-        )
+        places = [(u, 0, UNIT, key_end + KV_HEADS * HEAD_DIM + u * UNIT) for u in range(2)]
+        for j in range(pairs):
+            places.append((2 + j, 0, 2 * PAIR, 2 * j * PAIR))
+            places.append((2 + j, 2 * PAIR, PAIR, query_end + j * PAIR))
+            places.append((2 + j, 3 * PAIR, PAIR, key_end + j * PAIR))
+        small_columns[...] = small_totals[0].T
+        outs = [pltpu.make_async_copy(small_columns, small_hbm, out_sem.at[len(places)])]
+        for number, (u, at, size, column) in enumerate(places):
+            outs.append(
+                pltpu.make_async_copy(
+                    totals.at[u, :, at : at + size],
+                    sum_hbm.at[:, column : column + size],
+                    out_sem.at[number],
+                )
+            )
     else:
         outs = (
             pltpu.make_async_copy(own, sum_hbm, load_sem.at[3]),
@@ -1368,19 +1475,19 @@
             bank_total_copy(e).wait()
         for side in range(2):
 
-            @pl.when(z != side * (line - 1))
+            @pl.when(starts[1 - side])
             def _(side=side):
-                late_send(side, z).wait_send()
-
-            @pl.when(z == side * (line - 1))
-            def _():
                 mix_load(z).wait()
-                total = hidden[...] + mixes[z].astype(F32)
-                for step in range(1, line):
-                    source = lax.rem(z + step, line)
-                    late_send(0, source).wait_recv()
-                    total = total + mixes[source].astype(F32)
-                output[...] = total.astype(BF16)
+                for p in range(PIECES):
+                    chain_send(side, p, late_hbm).wait_recv()
+                output[...] = (
+                    hidden[...] + mixes[z].astype(F32) + chain_in[side].astype(F32)
+                ).astype(BF16)
+
+            @pl.when(jnp.logical_not(starts[1 - side]))
+            def _(side=side):
+                for p in range(PIECES):
+                    chain_send(side, p, late_hbm).wait_send()
 
     for copy in outs:
         copy.wait()
@@ -1397,7 +1504,7 @@
     held = pl.BlockSpec(memory_space=pltpu.VMEM)
     anywhere = pl.BlockSpec(memory_space=pl.ANY)
     if paired:
-        sum_shapes = (shape((units, rows, UNIT), F32), shape((1, rows, 128), F32))
+        sum_shapes = (shape((rows, units * UNIT), F32), shape((128, rows), F32))
     else:
         sum_shapes = (
             shape((units, 2, 2, 2, block_rows, UNIT), BF16),
@@ -1419,7 +1526,7 @@
             pltpu.SemaphoreType.DMA((3, units + 1)),
             pltpu.SemaphoreType.DMA((units + 1, line)),
             pltpu.SemaphoreType.DMA((units + 1, line)),
-            pltpu.SemaphoreType.DMA((2,)),
+            pltpu.SemaphoreType.DMA((3 + 3 * pairs,)),
         ]
         bank_shape = (far_args[5].shape[0],) + far_args[5].shape[2:]
         sum_shapes += (shape(bank_shape, F32),)
@@ -1428,8 +1535,12 @@
             pltpu.VMEM(bank_shape, BF16),
             pltpu.VMEM(bank_shape, F32),
             pltpu.SemaphoreType.DMA((4, bank_shape[0])),
+            pltpu.VMEM((128, rows), F32),
+            pltpu.VMEM((2, count, width), BF16),
+            pltpu.VMEM((2, count, width), BF16),
+            pltpu.VMEM((2, count, width), BF16),
             pltpu.SemaphoreType.DMA((2,)),
-            pltpu.SemaphoreType.DMA((line,)),
+            pltpu.SemaphoreType.DMA((2, 2, PIECES)),
         ]
     settings = dict(vmem_limit_bytes=VMEM_MOST)
     if paired:
@@ -1477,6 +1588,51 @@
         ),
         side_by_side(sums[:2]),
     )
+
+
+def update_kernel(width, experts, bank_sum, head_sum, small_rows, *refs):
+    lanes = refs[0].shape[2]
+    gradients = (
+        bank_sum[0, :, :lanes],
+        bank_sum[0, :, lanes:],
+        head_sum[:, :width],
+        head_sum[:, width:],
+        small_rows[:experts],
+        small_rows[experts : experts + 2],
+    )
+    count = len(gradients)
+    for number, gradient in enumerate(gradients):
+        held = refs[3 * number : 3 * number + 3]
+        results = refs[3 * (count + number) : 3 * (count + number) + 3]
+        at = (0,) if held[0].ndim == 3 else (Ellipsis,)
+        values = update(gradient, *(ref[at] for ref in held))
+        for ref, value in zip(results, values):
+            ref[at] = value
+
+
+def update_all(bank_sum, head_sum, small_rows, states):
+    experts, block_rows, _ = bank_sum.shape
+    half = block_rows // 2
+    rows = head_sum.shape[0] // experts
+
+    def spec(value):
+        if value.ndim == 3:
+            return pl.BlockSpec((1, half, value.shape[2]), lambda i: (i // 2, i % 2, 0))
+        if value.shape[0] == head_sum.shape[0] and value.shape[1] > 128:
+            return pl.BlockSpec((rows, value.shape[1]), lambda i: (i // 2, 0))
+        return pl.BlockSpec(value.shape, lambda i: (0, 0))
+
+    flat = [value for state in states for value in state]
+    results = pl.pallas_call(
+        functools.partial(update_kernel, states[2][0].shape[1], states[4][0].shape[0]),
+        grid=(2 * experts,),
+        out_shape=tuple(jax.ShapeDtypeStruct(value.shape, F32) for value in flat),
+        in_specs=[spec(value) for value in (bank_sum, head_sum, small_rows, *flat)],
+        out_specs=tuple(spec(value) for value in flat),
+        compiler_params=pltpu.CompilerParams(vmem_limit_bytes=VMEM_MOST),
+        cost_estimate=pl.CostEstimate(flops=2**23, bytes_accessed=25 * 2**20, transcendentals=0),
+    )(bank_sum, head_sum, small_rows, *flat)
+    return [tuple(results[i : i + 3]) for i in range(0, len(flat), 3)]
 
 
 def body(
@@ -1591,10 +1747,20 @@
         paired,
         peer_count,
     )
+    shard_rows = model_width // lax.axis_size(("dp", "expert"))
+    gains_share = lax.dynamic_slice_in_dim(
+        gain_rows, lax.axis_index(("dp", "expert")) * shard_rows, shard_rows, 1
+    )
+    states = (
+        (expert_in_master, expert_in_moment, expert_in_average),
+        (expert_out_master, expert_out_moment, expert_out_average),
+        (heads_in_master, heads_in_moment, heads_in_average),
+        (heads_out_master, heads_out_moment, heads_out_average),
+        (router_master.T, router_moment.T, router_average.T),
+        (gains_share, gains_moment.T, gains_average.T),
+    )
     if paired:
-        small_sum = small_sum[0]
-        cut = expert_in.shape[2]
-        expert_sums = (bank_sums[0][:, :, :cut], bank_sums[0][:, :, cut:])
+        news = update_all(bank_sums[0], unit_sums, small_sum, states)
     else:
         head_parts = unit_columns(unit_sums.reshape(unit_sums.shape[0], model_width, UNIT))
         packed = jnp.concatenate([*head_parts, small_sum.reshape(model_width, 128)], axis=1)
@@ -1603,32 +1769,18 @@
         ).astype(jnp.float32)
         cut_in = head_parts[0].shape[1]
         cut_out = cut_in + head_parts[1].shape[1]
-        head_parts = (head_total[:, :cut_in], head_total[:, cut_in:cut_out])
-        small_sum = head_total[:, cut_out:]
-    if paired:
-        head_parts = unit_columns(unit_sums)
-    head_in_sum, head_out_sum = head_parts
-    summed = (
-        head_in_sum,
-        head_out_sum,
-    )
-    shard_rows = model_width // lax.axis_size(("dp", "expert"))
-    small_rows = small_sum.T
-    gains_share = lax.dynamic_slice_in_dim(
-        gain_rows, lax.axis_index(("dp", "expert")) * shard_rows, shard_rows, 1
-    )
-    gains_new = update(
-        small_rows[experts : experts + 2], gains_share, gains_moment.T, gains_average.T
-    )
+        small_rows = head_total[:, cut_out:].T
+        sums = (
+            *expert_sums,
+            head_total[:, :cut_in],
+            head_total[:, cut_in:cut_out],
+            small_rows[:experts],
+            small_rows[experts : experts + 2],
+        )
+        news = [update(gradient, *state) for gradient, state in zip(sums, states)]
+    upper_new, lower_new, inproj_new, outproj_new, router_new, gains_new = news
+    router_new = tuple(value.T for value in router_new)
     gains_new = tuple(value.T for value in gains_new)
-    inproj_new = update(summed[0], heads_in_master, heads_in_moment, heads_in_average)
-    outproj_new = update(summed[1], heads_out_master, heads_out_moment, heads_out_average)
-    router_new = update(
-        small_rows[:experts], router_master.T, router_moment.T, router_average.T
-    )
-    router_new = tuple(value.T for value in router_new)
-    upper_new = update(expert_sums[0], expert_in_master, expert_in_moment, expert_in_average)
-    lower_new = update(expert_sums[1], expert_out_master, expert_out_moment, expert_out_average)
     return (
         output,
         token_grad,

time: 311 us -> 289 us (0.929)
  other arithmetic: 17.5 us -> 3.79 us
  local copies, waits for them, and re-layouts: 12.2 us -> 5.4 us
    add x4 -> x0, other arithmetic: 12.2 us -> none  [update(): DECAY * average + (1.0 - DECAY) * master_next]
    pallas_call x0 -> x1, Pallas kernels: none -> 11.8 us  [update_all(): pl.pallas_call(functools.partial(update_kernel, states[2][0].shape[1], st...]
    pallas_call x1, Pallas kernels: 76.3 us -> 66.3 us  [attend_back(): pl.pallas_call(functools.partial(attend_back_kernel, paired, line), out_s...]
    unnamed x53 -> x8, local copies, waits for them, and re-layouts: 9.93 us -> 2.8 us
    pallas_call x1, Pallas kernels: 132 us -> 129 us  [front(): pl.pallas_call(functools.partial(front_kernel, line, prompt, late), out_s...]
  transfers between devices with their start and end apart: 1 -> 1, of which waited for: 0 -> 0; matrix products, arithmetic and copies ran while one was open for 1% -> 1% of each run, Pallas kernels for 19% -> 20%
where the time goes in v2:
time: 289 us
  Pallas kernels  265 us (92%)
  between operations  14.2 us (5%)
  local copies, waits for them, and re-layouts  5.4 us (2%)
  other arithmetic  3.79 us (1%)
    pallas_call x1, Pallas kernels, front(): pl.pallas_call(functools.partial(front_kernel, line, prompt, late), out_s...  129 us
    pallas_call x1, Pallas kernels, attend_back(): pl.pallas_call(functools.partial(attend_back_kernel, paired, line), out_s...  66.3 us
    pallas_call x1, Pallas kernels, bank_grads(): pl.pallas_call(bank_grads_kernel, out_shape=jax.ShapeDtypeStruct((experts...  58.1 us
    pallas_call x1, Pallas kernels, update_all(): pl.pallas_call(functools.partial(update_kernel, states[2][0].shape[1], st...  11.8 us
  transfers between devices with their start and end apart: 1, of which 0 were waited for; matrix products, arithmetic and copies ran while one was open for 1% of the time, Pallas kernels for 20%

profile of v2, /device:TPU:0, one launch (start us, length us, event | category | flops | bytes accessed | tf_op | source)
XLA Modules:
  0.0 288.6 jit_solution(12062686881844032721)
XLA Ops:
  7.2 0.0 reduce-scatter.2.cloned.1.call-start
  7.3 0.9 convert_reduce_fusion
  8.2 0.7 concatenate.19
  8.9 0.8 fusion.2
  9.6 1.0 fusion.1.bias
  10.6 1.1 pad_maximum_fusion
  11.7 129.0 %shard_map.410 = (bf16[384,1024]{1,0:T(8,128)(2,1)}, bf16[384,1024]{1,0:T(8,128)(2,1)}, bf16[384,512]{1,0:T(8,128)(2,1)}, bf16[384,512]{1,0:T(8,128)(2,1)}, bf16...) custom-call(bf16[384,1024]{1,0:T(8,128)(2,1)} %tokens_hbm.1, ...), custom_call_target="tpu_custom_call" | custom-call | flops 34359738368 | bytes 67108864 | tf_op jit(solution)/shard_map/pallas_call | solution.py:893
  140.7 0.0 copy-start.2
  140.7 0.0 reduce-scatter.2.cloned.1.call-update
  140.8 0.8 copy-done.2
  141.5 0.6 reshape.87.gate_grads
  142.1 1.3 dynamic-slice_bitcast_fusion.refs_15_
  143.5 58.1 %shard_map.411.others_0_ = bf16[4,2,128,1536]{3,2,1,0:T(8,128)(2,1)} custom-call(bf16[1536,1024]{1,0:T(8,128)(2,1)} %bitcast.44, bf16[1536,1024]{1,0:T(8,128)(2,1)} %bitcast.43, bf16[1536,2048]{1,0:T(8,128)(2,1)} %bitcast.42, bf16[1536,4096]{1,0:T(8,128)(2,1)} %bitcast.41), custom_call_target="tpu_custom_call" | custom-call | flops 19327352832 | bytes 134217728 | tf_op jit(solution)/shard_map/pallas_call | solution.py:342
  201.6 0.0 reduce-scatter.2.cloned.1.call-done.back_rows
  201.6 66.3 %shard_map.412 = (bf16[384,1024]{1,0:T(8,128)(2,1)}, f32[384,1024]{1,0:T(8,128)}, f32[32,3072]{1,0:T(8,128)}, f32[128,32]{1,0:T(8,128)}, f32[4,128,1536]{2,1,0:T(8,128)}) custom-call(bf16[384,1024]{1,0:T(8,128)(2,1)} %reduce-scatter.2.cloned.1.call-done.back_rows, f32[384,1024]{1,0:T(8,128)} %get-tuple-element.61.hidden, bf16[384,1024]{1,0:T(8,128)(2,1)} %cots.1, ...), custom_call_target="tpu_custom_call" | custom-call | flops 17179869184 | bytes 33554432 | tf_op jit(solution)/shard_map/pallas_call | solution.py:1548
  267.9 0.0 copy-start.1
  267.9 0.0 copy-start
  267.9 11.8 %shard_map.413 = (f32[4,128,1024]{2,1,0:T(8,128)}, f32[4,128,1024]{2,1,0:T(8,128)}, f32[4,128,1024]{2,1,0:T(8,128)}, f32[4,128,512]{2,1,0:T(8,128)}, f32[4,128,5...) custom-call(f32[4,128,1536]{2,1,0:T(8,128)} %get-tuple-element.79.ba, ...), custom_call_target="tpu_custom_call" | custom-call | flops 8388608 | bytes 26214400 | tf_op jit(solution)/shard_map/pallas_call | solution.py:1626
  279.7 0.0 copy-done.1
  279.7 0.9 copy.50
  280.6 0.0 copy-done
  280.6 1.1 copy.51
  (8 shorter events, 0.0 us)
Async XLA Ops:
  7.2 194.4 %reduce-scatter.2.cloned.1.call-start = ((), (), s32[]{:S(2)}) async-start(), calls=%async_computation.1 | async-start | bytes 3932160 | tf_op jit(solution)/shard_map/reduce_scatter | solution.py:1709
  140.7 0.8 copy-start.2
  267.9 11.8 %copy-start.1 = (bf16[384,1024]{1,0:T(8,128)(2,1)S(1)}, bf16[384,1024]{1,0:T(8,128)(2,1)}, u32[]{:S(2)}) copy-start(bf16[384,1024]{1,0:T(8,128)(2,1)} %get-tuple-element.125) | copy-start | bytes 2359300
  267.9 12.7 %copy-start = (f32[384,1024]{1,0:T(8,128)S(1)}, f32[384,1024]{1,0:T(8,128)}, u32[]{:S(2)}) copy-start(f32[384,1024]{1,0:T(8,128)} %get-tuple-element.126) | copy-start | bytes 4718596
Sparse Core Ops, SparseCore 0:
  140.9 60.5 reduce-scatter.1

commit v3 on v2

--- a/solution.py
+++ b/solution.py
@@ -2,6 +2,7 @@
 
 import jax
 import jax.numpy as jnp
+import numpy as np
 from jax import lax
 from jax.experimental import pallas as pl
 from jax.experimental.pallas import tpu as pltpu
@@ -19,29 +20,6 @@
 DECAY = 0.8
 RATE = 0.001
 HIGHEST = lax.Precision.HIGHEST
-
-
-def layout(labels_row, prompt_len):
-    places = jnp.arange(prompt_len + labels_row.shape[0], dtype=jnp.int32)
-    earlier = jnp.sum((labels_row[None, :] < labels_row[:, None]).astype(jnp.int32), axis=1)
-    offset = places[prompt_len:] - prompt_len - earlier
-    positions = jnp.concatenate([places[:prompt_len], prompt_len + offset]).astype(jnp.float32)
-    labels = jnp.concatenate([jnp.full((prompt_len,), -1, jnp.int32), labels_row])
-    allowed = (places[None, :] <= places[:, None]) & (
-        (places[None, :] < prompt_len) | (labels[None, :] == labels[:, None])
-    )
-    return (positions, allowed)
-
-
-def rope_tables(positions):
-    middle = HEAD_DIM // 2
-    frequency = THETA ** (-2.0 * jnp.arange(middle, dtype=jnp.float32) / HEAD_DIM)
-    angles = positions[:, None] * frequency[None, :]
-    cosine, sine = jnp.cos(angles), jnp.sin(angles)
-    return (
-        jnp.concatenate([cosine] * 4, axis=1),
-        jnp.concatenate([-sine, sine, -sine, sine], axis=1),
-    )
 
 
 def update(gradient, master, moment, average):
@@ -411,9 +389,8 @@
     heads_out_hbm,
     router_rows,
     route_rows,
-    cosine,
-    sine,
-    bias,
+    label_row,
+    frequencies,
     up_hbm,
     down_hbm,
     first_in_hbm,
@@ -425,6 +402,9 @@
     second_in_hbm,
     gate_rows,
     log_totals,
+    cosine_hbm,
+    sine_hbm,
+    bias_hbm,
     cots_all,
     mix_all,
     mix_late,
@@ -469,6 +449,9 @@
     attended,
     hidden,
     second_in,
+    cosine,
+    sine,
+    bias,
     held_sem,
 ):
     dp = lax.axis_index("dp")
@@ -494,6 +477,9 @@
                 (attended, attended_hbm),
                 (hidden, hidden_hbm),
                 (second_in, second_in_hbm),
+                (cosine, cosine_hbm),
+                (sine, sine_hbm),
+                (bias, bias_hbm),
             )
         )
     ]
@@ -537,6 +523,24 @@
     own_cots = pltpu.make_async_copy(cots, cots_all.at[z], local_sem.at[0])
     own_cots.start()
 
+    labels = label_row[...].astype(F32)
+    size = labels.shape[1]
+    square = jnp.broadcast_to(labels, (size, size))
+    upright = square.T
+    earlier = jnp.sum(jnp.where(square < upright, 1.0, 0.0), axis=1, keepdims=True)
+    place = lax.broadcasted_iota(jnp.int32, (token_rows.shape[0], 128), 0).astype(F32)
+    shift = jnp.concatenate([jnp.zeros((prompt, 1), F32), earlier], axis=0)
+    angles = (place - shift) * frequencies[...]
+    lane = lax.broadcasted_iota(jnp.int32, angles.shape, 1)
+    sines = jnp.sin(angles)
+    cosine[...] = jnp.cos(angles)
+    sine[...] = jnp.where(lax.rem(lane, HEAD_DIM) < HEAD_DIM // 2, -sines, sines)
+    own_label = jnp.concatenate([jnp.full((prompt, 1), -1.0, F32), upright[:, :1]], axis=0)
+    seen_label = jnp.concatenate([jnp.full((1, prompt), -1.0, F32), labels], axis=1)
+    row = lax.broadcasted_iota(jnp.int32, bias.shape, 0)
+    column = lax.broadcasted_iota(jnp.int32, bias.shape, 1)
+    allowed = (column <= row) & ((column < prompt) | (own_label == seen_label))
+    bias[...] = jnp.where(allowed, 0.0, -1e30)
     heads_in_load.wait()
 
     def project(i, _):
@@ -875,7 +879,8 @@
     heads_out,
     router_rows,
     route_rows,
-    tables,
+    label_row,
+    frequencies,
     up,
     down,
     line,
@@ -902,6 +907,9 @@
             shape((count, width), BF16),
             shape((named, count), F32),
             shape((count, 128), F32),
+            shape((count, 128), F32),
+            shape((count, 128), F32),
+            shape((count, count), F32),
             shape((line, count, width), BF16),
             shape((line, count, width), BF16),
             shape((2, count, width), BF16),
@@ -911,8 +919,8 @@
             shape((line, count, experts * 2 * ff_width), BF16),
             shape((line, count, width), BF16),
         ),
-        in_specs=[held, anywhere, held, anywhere, anywhere] + [held] * 5 + [anywhere] * 2,
-        out_specs=(anywhere,) * 7 + (held,) * 2 + (anywhere,) * 8,
+        in_specs=[held, anywhere, held, anywhere, anywhere] + [held] * 4 + [anywhere] * 2,
+        out_specs=(anywhere,) * 7 + (held,) * 2 + (anywhere,) * 11,
         scratch_shapes=[
             pltpu.VMEM((count, width), BF16),
             pltpu.VMEM((line, count, width), BF16),
@@ -950,7 +958,10 @@
             pltpu.VMEM((count, HEADS * HEAD_DIM), BF16),
             pltpu.VMEM((count, width), F32),
             pltpu.VMEM((count, width), BF16),
-            pltpu.SemaphoreType.DMA((9,)),
+            pltpu.VMEM((count, 128), F32),
+            pltpu.VMEM((count, 128), F32),
+            pltpu.VMEM((count, count), F32),
+            pltpu.SemaphoreType.DMA((12,)),
         ],
         compiler_params=pltpu.CompilerParams(
             collective_id=4, has_side_effects=True, vmem_limit_bytes=VMEM_MOST
@@ -964,7 +975,8 @@
         heads_out,
         router_rows,
         route_rows,
-        *tables,
+        label_row,
+        frequencies,
         up,
         down,
     )
@@ -1005,6 +1017,7 @@
         first_in,
         heads_in,
         mixes,
+        gate_grad_rows,
         grad_hidden,
         grad_attended,
         grad_projected,
@@ -1288,7 +1301,10 @@
             ]
 
     gates = gate_rows[...]
-    gate_grad = gate_grads[...]
+    local = gates.shape[0] // line
+    for b in range(line):
+        gate_grad_rows[b * local : (b + 1) * local] = gate_grads[b, :local]
+    gate_grad = gate_grad_rows[...]
     logit_grad = gates * (gate_grad - jnp.sum(gates * gate_grad, axis=0, keepdims=True))
     high = logit_grad.astype(BF16)
     low = (logit_grad - high.astype(F32)).astype(BF16)
@@ -1451,6 +1467,13 @@
             places.append((2 + j, 2 * PAIR, PAIR, query_end + j * PAIR))
             places.append((2 + j, 3 * PAIR, PAIR, key_end + j * PAIR))
         small_columns[...] = small_totals[0].T
+        gain_values = gain_rows[...]
+        share = jnp.zeros((2, rows), F32)
+        for i in range(gain_values.shape[1] // rows):
+            share = jnp.where(
+                dp * line + z == i, gain_values[:, i * rows : (i + 1) * rows], share
+            )
+        small_columns[experts + 2 : experts + 4] = share
         outs = [pltpu.make_async_copy(small_columns, small_hbm, out_sem.at[len(places)])]
         for number, (u, at, size, column) in enumerate(places):
             outs.append(
@@ -1555,6 +1578,7 @@
             pltpu.VMEM((count, width), BF16),
             pltpu.VMEM(heads_in.shape, BF16),
             pltpu.VMEM((line, count, width), BF16),
+            pltpu.VMEM(held_args[4].shape, F32),
             pltpu.VMEM((count, width), F32),
             pltpu.VMEM((count, HEADS * HEAD_DIM), BF16),
             pltpu.VMEM((pairs, count, 4 * PAIR), BF16),
@@ -1603,6 +1627,8 @@
     count = len(gradients)
     for number, gradient in enumerate(gradients):
         held = refs[3 * number : 3 * number + 3]
+        if number == count - 1:
+            held = (small_rows.at[experts + 2 : experts + 4], *held[1:])
         results = refs[3 * (count + number) : 3 * (count + number) + 3]
         at = (0,) if held[0].ndim == 3 else (Ellipsis,)
         values = update(gradient, *(ref[at] for ref in held))
@@ -1669,8 +1695,9 @@
     peer_count = lax.axis_size("expert")
     experts = local_experts * peer_count
     paired = lax.axis_size("dp") == 8 and peer_count == 4
-    positions, allowed = layout(cont_ids[0], token_count - cont_ids.shape[1])
-    tables = (*rope_tables(positions), jnp.where(allowed, 0.0, -1e30))
+    half = HEAD_DIM // 2
+    powers = [THETA ** (-2.0 * (lane % half) / HEAD_DIM) for lane in range(128)]
+    frequencies = jnp.asarray(np.array(powers, np.float32)[None])
     gain_rows = norm_gains.T
     router_rows = router.T
     (
@@ -1683,6 +1710,9 @@
         second_in,
         gates,
         log_totals,
+        cosine,
+        sine,
+        bias,
         cots_all,
         mix_all,
         mix_late,
@@ -1700,7 +1730,8 @@
         heads_out,
         router_rows,
         routes.T,
-        tables,
+        cont_ids,
+        frequencies,
         expert_in,
         expert_out,
         peer_count,
@@ -1732,7 +1763,7 @@
             cotangent,
             second_in,
             gates,
-            gate_grads[:, :local_experts].reshape(experts, token_count),
+            gate_grads,
             router_rows,
             gain_rows,
             heads_out,
@@ -1741,16 +1772,21 @@
             value_rows,
             attended,
             log_totals,
-            *tables,
+            cosine,
+            sine,
+            bias,
         ),
         (tokens, first_in, heads_in, mix_all, mix_late, *(expert_sums if paired else ())),
         paired,
         peer_count,
     )
-    shard_rows = model_width // lax.axis_size(("dp", "expert"))
-    gains_share = lax.dynamic_slice_in_dim(
-        gain_rows, lax.axis_index(("dp", "expert")) * shard_rows, shard_rows, 1
-    )
+    if paired:
+        gains_share = gains_moment.T
+    else:
+        shard_rows = model_width // lax.axis_size(("dp", "expert"))
+        gains_share = lax.dynamic_slice_in_dim(
+            gain_rows, lax.axis_index(("dp", "expert")) * shard_rows, shard_rows, 1
+        )
     states = (
         (expert_in_master, expert_in_moment, expert_in_average),
         (expert_out_master, expert_out_moment, expert_out_average),

time: 289 us -> 285 us (0.986)
  other arithmetic: 3.79 us -> 0 us
  local copies, waits for them, and re-layouts: 5.4 us -> 2.03 us
  transfers between devices with their start and end apart: 1 -> 1, of which waited for: 0 -> 1; matrix products, arithmetic and copies ran while one was open for 1% -> 0% of each run, Pallas kernels for 20% -> 20%
where the time goes in v3:
time: 285 us
  Pallas kernels  266 us (93%)
  between operations  14.1 us (5%)
    pallas_call x1, Pallas kernels, front(): pl.pallas_call(functools.partial(front_kernel, line, prompt, late), out_s...  129 us
    pallas_call x1, Pallas kernels, attend_back(): pl.pallas_call(functools.partial(attend_back_kernel, paired, line), out_s...  66.7 us
    pallas_call x1, Pallas kernels, bank_grads(): pl.pallas_call(bank_grads_kernel, out_shape=jax.ShapeDtypeStruct((experts...  58.2 us
    pallas_call x1, Pallas kernels, update_all(): pl.pallas_call(functools.partial(update_kernel, states[2][0].shape[1], st...  11.8 us
  transfers between devices with their start and end apart: 1, of which 1 were waited for; matrix products, arithmetic and copies ran while one was open for 0% of the time, Pallas kernels for 20%

profile of v3, /device:TPU:0, one launch (start us, length us, event | category | flops | bytes accessed | tf_op | source)
XLA Modules:
  0.0 284.7 jit_solution(9678214487065540379)
XLA Ops:
  7.2 0.0 reduce-scatter.2.cloned.1.call-start
  7.2 129.3 %shard_map.419 = (bf16[384,1024]{1,0:T(8,128)(2,1)}, bf16[384,1024]{1,0:T(8,128)(2,1)}, bf16[384,512]{1,0:T(8,128)(2,1)}, bf16[384,512]{1,0:T(8,128)(2,1)}, bf16...) custom-call(bf16[384,1024]{1,0:T(8,128)(2,1)} %tokens_hbm.1, ...), custom_call_target="tpu_custom_call" | custom-call | flops 34359738368 | bytes 67108864 | tf_op jit(solution)/shard_map/pallas_call | solution.py:898
  136.6 0.0 reduce-scatter.2.cloned.1.call-update
  136.6 58.2 %shard_map.420.others_0_ = bf16[4,2,128,1536]{3,2,1,0:T(8,128)(2,1)} custom-call(bf16[1536,1024]{1,0:T(8,128)(2,1)} %bitcast.40, bf16[1536,1024]{1,0:T(8,128)(2,1)} %bitcast.39, bf16[1536,2048]{1,0:T(8,128)(2,1)} %bitcast.38, bf16[1536,4096]{1,0:T(8,128)(2,1)} %bitcast.37), custom_call_target="tpu_custom_call" | custom-call | flops 19327352832 | bytes 134217728 | tf_op jit(solution)/shard_map/pallas_call | solution.py:320
  194.8 2.5 reduce-scatter.2.cloned.1.call-done.back_rows
  197.3 66.7 %shard_map.421 = (bf16[384,1024]{1,0:T(8,128)(2,1)}, f32[384,1024]{1,0:T(8,128)}, f32[32,3072]{1,0:T(8,128)}, f32[128,32]{1,0:T(8,128)}, f32[4,128,1536]{2,1,0:T(8,128)}) custom-call(bf16[384,1024]{1,0:T(8,128)(2,1)} %reduce-scatter.2.cloned.1.call-done.back_rows, f32[384,1024]{1,0:T(8,128)} %get-tuple-element.64.hidden, bf16[384,1024]{1,0:T(8,128)(2,1)} %cots.1, ...), custom_call_target="tpu_custom_call" | custom-call | flops 17179869184 | bytes 33554432 | tf_op jit(solution)/shard_map/pallas_call | solution.py:1571
  264.0 0.0 copy-start.1
  264.0 0.0 copy-start
  264.0 11.8 %shard_map.422 = (f32[4,128,1024]{2,1,0:T(8,128)}, f32[4,128,1024]{2,1,0:T(8,128)}, f32[4,128,1024]{2,1,0:T(8,128)}, f32[4,128,512]{2,1,0:T(8,128)}, f32[4,128,5...) custom-call(f32[4,128,1536]{2,1,0:T(8,128)} %get-tuple-element.85.ba, ...), custom_call_target="tpu_custom_call" | custom-call | flops 8388608 | bytes 26214400 | tf_op jit(solution)/shard_map/pallas_call | solution.py:1652
  275.8 0.0 copy-done.1
  275.9 0.9 copy.50
  276.7 0.0 copy-done
  276.7 1.1 copy.51
Async XLA Ops:
  7.2 190.1 %reduce-scatter.2.cloned.1.call-start = ((), (), s32[]{:S(2)}) async-start(), calls=%async_computation.1 | async-start | bytes 3932160 | tf_op jit(solution)/shard_map/reduce_scatter | solution.py:1740
  264.0 11.8 %copy-start.1 = (bf16[384,1024]{1,0:T(8,128)(2,1)S(1)}, bf16[384,1024]{1,0:T(8,128)(2,1)}, u32[]{:S(2)}) copy-start(bf16[384,1024]{1,0:T(8,128)(2,1)} %get-tuple-element.126) | copy-start | bytes 2359300
  264.0 12.7 %copy-start = (f32[384,1024]{1,0:T(8,128)S(1)}, f32[384,1024]{1,0:T(8,128)}, u32[]{:S(2)}) copy-start(f32[384,1024]{1,0:T(8,128)} %get-tuple-element.127) | copy-start | bytes 4718596
Sparse Core Ops, SparseCore 0:
  136.7 60.5 reduce-scatter.1

commit v4 on v3

--- a/solution.py
+++ b/solution.py
@@ -453,6 +453,7 @@
     sine,
     bias,
     held_sem,
+    row_out_sem,
 ):
     dp = lax.axis_index("dp")
     z = lax.axis_index("expert")
@@ -661,6 +662,9 @@
             device_id_type=MESH,
         )
 
+    def row_out(block):
+        return pltpu.make_async_copy(rows.at[block], rows_all_hbm.at[block], row_out_sem.at[block])
+
     def own_mix():
         return pltpu.make_async_copy(mix_stage.at[z], mix_all.at[z], local_sem.at[3])
 
@@ -775,6 +779,7 @@
             return 0
 
         lax.fori_loop(0, 2, half, 0)
+        row_out(block).start()
         mix_stage[block] = contract(gated[slot], down[...], 1, 1).astype(BF16)
 
         @pl.when(block == z)
@@ -860,14 +865,11 @@
                 device_id_type=MESH,
             ).wait_recv()
 
-    last = (
-        pltpu.make_async_copy(rows, rows_all_hbm, local_sem.at[0]),
-        pltpu.make_async_copy(gate_grads, gate_grads_hbm, local_sem.at[1]),
-    )
-    for copy in last:
-        copy.start()
-    for copy in last:
-        copy.wait()
+    last = pltpu.make_async_copy(gate_grads, gate_grads_hbm, local_sem.at[1])
+    last.start()
+    for s in range(line):
+        row_out(s).wait()
+    last.wait()
 
 
 def front(
@@ -962,6 +964,7 @@
             pltpu.VMEM((count, 128), F32),
             pltpu.VMEM((count, count), F32),
             pltpu.SemaphoreType.DMA((12,)),
+            pltpu.SemaphoreType.DMA((line,)),
         ],
         compiler_params=pltpu.CompilerParams(
             collective_id=4, has_side_effects=True, vmem_limit_bytes=VMEM_MOST
@@ -1409,6 +1412,8 @@
         relay_on(False, 2)
         wide_sums.after_first(2)
         wide_sums.after_last(0)
+        wide_sums.after_first(3)
+        wide_sums.after_last(1)
     loads[1].wait()
     loads[2].wait()
     grad_first = jnp.zeros(grad_hidden.shape, F32)
@@ -1428,6 +1433,13 @@
     keep(own_small, 0, small_rows[...].T.astype(BF16))
     if paired:
         small_sum.core_send(0).start()
+    if paired:
+        wide_sums.after_first(4)
+        wide_sums.after_last(2)
+        small_sum.after_core(0)
+        wide_sums.after_first(5)
+        wide_sums.after_last(3)
+        small_sum.after_first(0)
     token_grad[...] = grad_hidden[...] + norm_grad
     if paired:
         for e in range(bank_hbm.shape[0]):
@@ -1445,20 +1457,10 @@
         output[...] = total.astype(BF16)
 
     if paired:
-        small_sum.after_core(0)
-        wide_sums.after_first(3)
-        wide_sums.after_last(1)
-        wide_sums.after_first(4)
-        wide_sums.after_last(2)
-        small_sum.after_first(0)
-        wide_sums.after_first(5)
-        wide_sums.after_last(3)
+        wide_sums.after_last(4)
         small_sum.after_last(0)
-        wide_sums.after_line(0)
-        wide_sums.after_last(4)
-        wide_sums.after_line(1)
         wide_sums.after_last(5)
-        for u in range(2, units):
+        for u in range(units):
             wide_sums.after_line(u)
         small_sum.after_line(0)
         places = [(u, 0, UNIT, key_end + KV_HEADS * HEAD_DIM + u * UNIT) for u in range(2)]
@@ -1638,20 +1640,19 @@
 
 def update_all(bank_sum, head_sum, small_rows, states):
     experts, block_rows, _ = bank_sum.shape
-    half = block_rows // 2
     rows = head_sum.shape[0] // experts
 
     def spec(value):
         if value.ndim == 3:
-            return pl.BlockSpec((1, half, value.shape[2]), lambda i: (i // 2, i % 2, 0))
+            return pl.BlockSpec((1, block_rows, value.shape[2]), lambda i: (i, 0, 0))
         if value.shape[0] == head_sum.shape[0] and value.shape[1] > 128:
-            return pl.BlockSpec((rows, value.shape[1]), lambda i: (i // 2, 0))
+            return pl.BlockSpec((rows, value.shape[1]), lambda i: (i, 0))
         return pl.BlockSpec(value.shape, lambda i: (0, 0))
 
     flat = [value for state in states for value in state]
     results = pl.pallas_call(
         functools.partial(update_kernel, states[2][0].shape[1], states[4][0].shape[0]),
-        grid=(2 * experts,),
+        grid=(experts,),
         out_shape=tuple(jax.ShapeDtypeStruct(value.shape, F32) for value in flat),
         in_specs=[spec(value) for value in (bank_sum, head_sum, small_rows, *flat)],
         out_specs=tuple(spec(value) for value in flat),

time: 285 us -> 282 us (0.989)
  Pallas kernels: 266 us -> 263 us
  transfers between devices with their start and end apart: 1 -> 1, of which waited for: 1 -> 1; matrix products, arithmetic and copies ran while one was open for 0% -> 0% of each run, Pallas kernels for 20% -> 21%
where the time goes in v4:
time: 282 us
  Pallas kernels  263 us (93%)
  between operations  14.1 us (5%)
    pallas_call x1, Pallas kernels, front(): pl.pallas_call(functools.partial(front_kernel, line, prompt, late), out_s...  128 us
    pallas_call x1, Pallas kernels, attend_back(): pl.pallas_call(functools.partial(attend_back_kernel, paired, line), out_s...  66.2 us
    pallas_call x1, Pallas kernels, bank_grads(): pl.pallas_call(bank_grads_kernel, out_shape=jax.ShapeDtypeStruct((experts...  58.2 us
    pallas_call x1, Pallas kernels, update_all(): pl.pallas_call(functools.partial(update_kernel, states[2][0].shape[1], st...  10.2 us
  transfers between devices with their start and end apart: 1, of which 1 were waited for; matrix products, arithmetic and copies ran while one was open for 0% of the time, Pallas kernels for 21%

profile of v4, /device:TPU:0, one launch (start us, length us, event | category | flops | bytes accessed | tf_op | source)
XLA Modules:
  0.0 281.7 jit_solution(6710908188153898674)
XLA Ops:
  7.2 0.0 reduce-scatter.2.cloned.1.call-start
  7.2 128.4 %shard_map.419 = (bf16[384,1024]{1,0:T(8,128)(2,1)}, bf16[384,1024]{1,0:T(8,128)(2,1)}, bf16[384,512]{1,0:T(8,128)(2,1)}, bf16[384,512]{1,0:T(8,128)(2,1)}, bf16...) custom-call(bf16[384,1024]{1,0:T(8,128)(2,1)} %tokens_hbm.1, ...), custom_call_target="tpu_custom_call" | custom-call | flops 34359738368 | bytes 67108864 | tf_op jit(solution)/shard_map/pallas_call | solution.py:900
  135.6 0.0 reduce-scatter.2.cloned.1.call-update
  135.6 58.2 %shard_map.420.others_0_ = bf16[4,2,128,1536]{3,2,1,0:T(8,128)(2,1)} custom-call(bf16[1536,1024]{1,0:T(8,128)(2,1)} %bitcast.40, bf16[1536,1024]{1,0:T(8,128)(2,1)} %bitcast.39, bf16[1536,2048]{1,0:T(8,128)(2,1)} %bitcast.38, bf16[1536,4096]{1,0:T(8,128)(2,1)} %bitcast.37), custom_call_target="tpu_custom_call" | custom-call | flops 19327352832 | bytes 134217728 | tf_op jit(solution)/shard_map/pallas_call | solution.py:320
  193.8 2.5 reduce-scatter.2.cloned.1.call-done.back_rows
  196.3 66.2 %shard_map.421 = (bf16[384,1024]{1,0:T(8,128)(2,1)}, f32[384,1024]{1,0:T(8,128)}, f32[32,3072]{1,0:T(8,128)}, f32[128,32]{1,0:T(8,128)}, f32[4,128,1536]{2,1,0:T(8,128)}) custom-call(bf16[384,1024]{1,0:T(8,128)(2,1)} %reduce-scatter.2.cloned.1.call-done.back_rows, f32[384,1024]{1,0:T(8,128)} %get-tuple-element.64.hidden, bf16[384,1024]{1,0:T(8,128)(2,1)} %cots.1, ...), custom_call_target="tpu_custom_call" | custom-call | flops 17179869184 | bytes 33554432 | tf_op jit(solution)/shard_map/pallas_call | solution.py:1573
  262.6 0.0 copy-start.1
  262.6 0.0 copy-start
  262.6 10.2 %shard_map.422 = (f32[4,128,1024]{2,1,0:T(8,128)}, f32[4,128,1024]{2,1,0:T(8,128)}, f32[4,128,1024]{2,1,0:T(8,128)}, f32[4,128,512]{2,1,0:T(8,128)}, f32[4,128,5...) custom-call(f32[4,128,1536]{2,1,0:T(8,128)} %get-tuple-element.85.ba, ...), custom_call_target="tpu_custom_call" | custom-call | flops 8388608 | bytes 26214400 | tf_op jit(solution)/shard_map/pallas_call | solution.py:1653
  272.8 0.0 copy-done.1
  272.8 0.9 copy.50
  273.7 0.0 copy-done
  273.7 1.1 copy.51
Async XLA Ops:
  7.2 189.1 %reduce-scatter.2.cloned.1.call-start = ((), (), s32[]{:S(2)}) async-start(), calls=%async_computation.1 | async-start | bytes 3932160 | tf_op jit(solution)/shard_map/reduce_scatter | solution.py:1741
  262.6 10.2 %copy-start.1 = (bf16[384,1024]{1,0:T(8,128)(2,1)S(1)}, bf16[384,1024]{1,0:T(8,128)(2,1)}, u32[]{:S(2)}) copy-start(bf16[384,1024]{1,0:T(8,128)(2,1)} %get-tuple-element.126) | copy-start | bytes 2359300
  262.6 11.1 %copy-start = (f32[384,1024]{1,0:T(8,128)S(1)}, f32[384,1024]{1,0:T(8,128)}, u32[]{:S(2)}) copy-start(f32[384,1024]{1,0:T(8,128)} %get-tuple-element.127) | copy-start | bytes 4718596
Sparse Core Ops, SparseCore 0:
  135.7 60.5 reduce-scatter.1

commit v5 on v4

--- a/solution.py
+++ b/solution.py
@@ -996,10 +996,10 @@
     gate_grads,
     router_rows,
     gain_rows,
-    heads_out,
-    queries,
-    keys,
-    values,
+    heads_out_hbm,
+    queries_hbm,
+    keys_hbm,
+    values_hbm,
     attended,
     log_totals,
     cosine,
@@ -1027,6 +1027,11 @@
         small_rows,
         own,
         own_small,
+        heads_out,
+        queries,
+        keys,
+        values,
+        held_sem,
         *scratch,
     ) = others
     dp = lax.axis_index("dp")
@@ -1039,6 +1044,19 @@
         pltpu.make_async_copy(tokens_hbm, tokens, load_sem.at[1]),
         pltpu.make_async_copy(in_hbm, heads_in, load_sem.at[2]),
     )
+    held_loads = [
+        pltpu.make_async_copy(source, target, held_sem.at[number])
+        for number, (source, target) in enumerate(
+            (
+                (heads_out_hbm, heads_out),
+                (queries_hbm, queries),
+                (keys_hbm, keys),
+                (values_hbm, values),
+            )
+        )
+    ]
+    for copy in held_loads:
+        copy.start()
     for copy in loads:
         copy.start()
 
@@ -1340,6 +1358,8 @@
         )
         if paired:
             wide_sums.core_send(u).start()
+    for copy in held_loads:
+        copy.wait()
     grad_attended[...] = contract(branch, heads_out[...], 1, 0).astype(BF16)
     loads[0].wait()
     if paired:
@@ -1573,7 +1593,8 @@
     return pl.pallas_call(
         functools.partial(attend_back_kernel, paired, line),
         out_shape=(shape((count, width), BF16), shape((count, width), F32)) + sum_shapes,
-        in_specs=[held] * len(held_args) + [anywhere] * len(far_args),
+        in_specs=[anywhere if 8 <= i < 12 else held for i in range(len(held_args))]
+        + [anywhere] * len(far_args),
         out_specs=(held, held) + (anywhere,) * len(sum_shapes),
         scratch_shapes=[
             pltpu.VMEM((count, width), BF16),
@@ -1587,6 +1608,8 @@
             pltpu.VMEM((128, width), F32),
             pltpu.VMEM((units, 2, 2, 2, block_rows, UNIT), BF16),
             pltpu.VMEM((1, 2, 2, 2, block_rows, 128), BF16),
+            *[pltpu.VMEM(value.shape, BF16) for value in held_args[8:12]],
+            pltpu.SemaphoreType.DMA((4,)),
             pltpu.SemaphoreType.DMA((5 + line,)),
             *exchange,
         ],

time: 282 us -> 281 us (level)
  no operation moved by 1% of the time
where the time goes in v5:
time: 281 us
  Pallas kernels  262 us (93%)
  between operations  14.1 us (5%)
    pallas_call x1, Pallas kernels, front(): pl.pallas_call(functools.partial(front_kernel, line, prompt, late), out_s...  128 us
    pallas_call x1, Pallas kernels, attend_back(): pl.pallas_call(functools.partial(attend_back_kernel, paired, line), out_s...  65.2 us
    pallas_call x1, Pallas kernels, bank_grads(): pl.pallas_call(bank_grads_kernel, out_shape=jax.ShapeDtypeStruct((experts...  58.2 us
    pallas_call x1, Pallas kernels, update_all(): pl.pallas_call(functools.partial(update_kernel, states[2][0].shape[1], st...  10.2 us
  transfers between devices with their start and end apart: 1, of which 1 were waited for; matrix products, arithmetic and copies ran while one was open for 0% of the time, Pallas kernels for 21%

profile of v5, /device:TPU:0, one launch (start us, length us, event | category | flops | bytes accessed | tf_op | source)
XLA Modules:
  0.0 280.7 jit_solution(2166701580661611178)
XLA Ops:
  7.2 0.0 reduce-scatter.2.cloned.1.call-start
  7.2 128.4 %shard_map.419 = (bf16[384,1024]{1,0:T(8,128)(2,1)}, bf16[384,1024]{1,0:T(8,128)(2,1)}, bf16[384,512]{1,0:T(8,128)(2,1)}, bf16[384,512]{1,0:T(8,128)(2,1)}, bf16...) custom-call(bf16[384,1024]{1,0:T(8,128)(2,1)} %tokens_hbm.1, ...), custom_call_target="tpu_custom_call" | custom-call | flops 34359738368 | bytes 67108864 | tf_op jit(solution)/shard_map/pallas_call | solution.py:900
  135.6 0.0 reduce-scatter.2.cloned.1.call-update
  135.6 58.2 %shard_map.420.others_0_ = bf16[4,2,128,1536]{3,2,1,0:T(8,128)(2,1)} custom-call(bf16[1536,1024]{1,0:T(8,128)(2,1)} %bitcast.40, bf16[1536,1024]{1,0:T(8,128)(2,1)} %bitcast.39, bf16[1536,2048]{1,0:T(8,128)(2,1)} %bitcast.38, bf16[1536,4096]{1,0:T(8,128)(2,1)} %bitcast.37), custom_call_target="tpu_custom_call" | custom-call | flops 19327352832 | bytes 134217728 | tf_op jit(solution)/shard_map/pallas_call | solution.py:320
  193.8 2.5 reduce-scatter.2.cloned.1.call-done.back_rows
  196.3 65.2 %shard_map.421 = (bf16[384,1024]{1,0:T(8,128)(2,1)}, f32[384,1024]{1,0:T(8,128)}, f32[32,3072]{1,0:T(8,128)}, f32[128,32]{1,0:T(8,128)}, f32[4,128,1536]{2,1,0:T(8,128)}) custom-call(bf16[384,1024]{1,0:T(8,128)(2,1)} %reduce-scatter.2.cloned.1.call-done.back_rows, f32[384,1024]{1,0:T(8,128)} %get-tuple-element.64.hidden, bf16[384,1024]{1,0:T(8,128)(2,1)} %cots.1, ...), custom_call_target="tpu_custom_call" | custom-call | flops 17179869184 | bytes 33554432 | tf_op jit(solution)/shard_map/pallas_call | solution.py:1593
  261.6 0.0 copy-start.1
  261.6 0.0 copy-start
  261.6 10.2 %shard_map.422 = (f32[4,128,1024]{2,1,0:T(8,128)}, f32[4,128,1024]{2,1,0:T(8,128)}, f32[4,128,1024]{2,1,0:T(8,128)}, f32[4,128,512]{2,1,0:T(8,128)}, f32[4,128,5...) custom-call(f32[4,128,1536]{2,1,0:T(8,128)} %get-tuple-element.85.ba, ...), custom_call_target="tpu_custom_call" | custom-call | flops 8388608 | bytes 26214400 | tf_op jit(solution)/shard_map/pallas_call | solution.py:1676
  271.8 0.0 copy-done.1
  271.8 0.9 copy.50
  272.7 0.0 copy-done
  272.7 1.1 copy.51
Async XLA Ops:
  7.2 189.1 %reduce-scatter.2.cloned.1.call-start = ((), (), s32[]{:S(2)}) async-start(), calls=%async_computation.1 | async-start | bytes 3932160 | tf_op jit(solution)/shard_map/reduce_scatter | solution.py:1764
  261.6 10.2 %copy-start.1 = (bf16[384,1024]{1,0:T(8,128)(2,1)S(1)}, bf16[384,1024]{1,0:T(8,128)(2,1)}, u32[]{:S(2)}) copy-start(bf16[384,1024]{1,0:T(8,128)(2,1)} %get-tuple-element.126) | copy-start | bytes 2359300
  261.6 11.1 %copy-start = (f32[384,1024]{1,0:T(8,128)S(1)}, f32[384,1024]{1,0:T(8,128)}, u32[]{:S(2)}) copy-start(f32[384,1024]{1,0:T(8,128)} %get-tuple-element.127) | copy-start | bytes 4718596
Sparse Core Ops, SparseCore 0:
  135.7 60.5 reduce-scatter.1
